TPU v7x, 128 devices: a whole 4x4x4 slice. The times are simulated.
128 devices in a mesh: row: 8 (over y_lo, x), col: 16 (over y_hi, z, core).
Axes of the slice: x: 4, y: 4 (y_hi: 2, y_lo: 2; y = y_hi * 2 + y_lo), z: 4, core: 2. Of those that a mesh axis runs over, the one named last changes fastest.
Arguments:
- factor_panel: bfloat16 [12288, 98304], P('row', 'col'), may hold values from -1 to 1, as said below
- normals: bfloat16 [98304, 128], P(('col', 'row')), may hold values from -6 to 6
- bond_vectors: float32 [3, 4096, 12], P(None, ('col', 'row')), may hold values from -9 to 9
- neighbours: int32 [4096, 12], P(('col', 'row')), may hold values from 0 to 175
- send_atoms: int32 [128, 16], P(('col', 'row')), may hold values from 0 to 31
- radial_weight: bfloat16 [128, 128], replicated, may hold values from -1.5 to 1.5
- radial_bias: float32 [128], replicated, may hold values from -3 to 3
- middle_weight: bfloat16 [128, 128], replicated, may hold values from -0.5 to 0.5
- middle_bias: float32 [128], replicated, may hold values from -3 to 3
- output_weight: float32 [128], replicated, may hold values from -0.5 to 0.5
Outputs:
- atom_energy: float32 [4096, 128], P(('col', 'row'))
- forces: float32 [3, 4096, 128], P(None, ('col', 'row'))
Inputs may be any that keep to these rules, and one draw needn't show every extreme that they name: `factor_panel`: entries above the factor's diagonal are zero.
All inputs are finite; a program needn't handle non-finite values.
Results may differ from a plain program's by a relative error of at most 0.0052.
Values may be sent and summed in bfloat16 or wider, within the bound.
A program may use at most 128 MiB of HBM per device.

v0:
```python
import jax
import jax.numpy as jnp
from jax import lax
from jax.sharding import PartitionSpec as P

TILE = 16


def with_halo(cells, sides, width):
    for axis, dim in sides:
        count = lax.axis_size(axis)
        head = lax.slice_in_dim(cells, 0, width, axis=dim)
        tail = lax.slice_in_dim(cells, cells.shape[dim] - width, cells.shape[dim], axis=dim)
        cells = jnp.concatenate(
            [
                lax.ppermute(tail, axis, [(i, (i + 1) % count) for i in range(count)]),
                cells,
                lax.ppermute(head, axis, [((i + 1) % count, i) for i in range(count)]),
            ],
            axis=dim,
        )
    return cells


def pair_terms(
    own_disp,
    near_disp,
    bond_block,
    radial_weight,
    radial_bias,
    middle_weight,
    middle_bias,
    output_weight,
):
    vectors = bond_block[:, :, :, None] + near_disp - own_disp[:, :, None, :]
    squared = jnp.sum(vectors * vectors, axis=0)
    count = radial_weight.shape[0]
    centres = 30.0 * jnp.arange(count, dtype=jnp.float32) / (count - 1)
    spread = 90.0 / (count - 1)
    scaled = (squared[..., None] - centres) / spread
    basis = jnp.exp(-scaled * scaled)
    flat_basis = basis.reshape(-1, count)
    flat_scaled = scaled.reshape(-1, count)
    first = jnp.tanh(
        jnp.dot(flat_basis.astype(jnp.bfloat16), radial_weight, preferred_element_type=jnp.float32)
        + radial_bias
    )
    second = jnp.tanh(
        jnp.dot(first.astype(jnp.bfloat16), middle_weight, preferred_element_type=jnp.float32)
        + middle_bias
    )
    energies = jnp.sum(second * output_weight, axis=-1)
    back_second = ((1.0 - second * second) * output_weight).astype(jnp.bfloat16)
    back_first = (
        jnp.dot(back_second, middle_weight.T, preferred_element_type=jnp.float32)
        * (1.0 - first * first)
    ).astype(jnp.bfloat16)
    radial_grad = jnp.dot(back_first, radial_weight.T, preferred_element_type=jnp.float32)
    slopes = jnp.sum(radial_grad * flat_basis * (-2.0 / spread) * flat_scaled, axis=-1)
    shape = squared.shape
    atom_part = 0.5 * jnp.sum(energies.reshape(shape), axis=1)
    force_part = 2.0 * jnp.sum(slopes.reshape(shape)[None] * vectors, axis=2)
    return (atom_part, force_part)


def per_device(
    factor_panel,
    normals,
    bond_vectors,
    neighbours,
    send_atoms,
    radial_weight,
    radial_bias,
    middle_weight,
    middle_bias,
    output_weight,
):
    samples = normals.shape[1]
    local_rows = factor_panel.shape[0]
    partial_value = jnp.dot(
        factor_panel,
        lax.all_gather(normals, "row", axis=0, tiled=True),
        preferred_element_type=jnp.float32,
    )
    col_count = lax.axis_size("col")
    col_index = lax.axis_index("col")
    slab_rows = local_rows // col_count
    total = lax.psum(partial_value, "col")
    slab = lax.dynamic_slice_in_dim(total, col_index * slab_rows, slab_rows, 0)
    rows_count = lax.axis_size("row")
    row_index = lax.axis_index("row")
    tiles = slab_rows // TILE
    whole = lax.all_gather(slab, "row", axis=0, tiled=True)
    ordered = (
        whole.reshape(rows_count, tiles, TILE, samples)
        .transpose(1, 0, 2, 3)
        .reshape(rows_count * slab_rows, samples)
    )
    domain = lax.dynamic_slice_in_dim(ordered, row_index * slab_rows, slab_rows, 0)
    domain_atoms = bond_vectors.shape[1]
    neighbour_count = bond_vectors.shape[2]
    displacements = domain.reshape(3, domain_atoms, samples)
    sent = jnp.take(displacements, send_atoms[0], axis=1)
    beside_all = with_halo(sent[None, None], (("row", 0), ("col", 1)), 1)
    halo_atoms = jnp.moveaxis(beside_all, 2, 0).reshape(3, 9 * sent.shape[1], samples)
    pool = jnp.concatenate([displacements, halo_atoms], axis=1)
    nearby = jnp.take(pool, neighbours.reshape(-1), axis=1).reshape(
        3, domain_atoms, neighbour_count, samples
    )
    block_count = domain_atoms // 8
    own_blocks = displacements.reshape(3, block_count, 8, samples).transpose(1, 0, 2, 3)
    near_blocks = nearby.reshape(3, block_count, 8, neighbour_count, samples).transpose(
        1, 0, 2, 3, 4
    )
    bond_blocks = bond_vectors.reshape(3, block_count, 8, neighbour_count).transpose(1, 0, 2, 3)
    energy_blocks, force_blocks = lax.map(
        lambda items: pair_terms(
            items[0],
            items[1],
            items[2],
            radial_weight,
            radial_bias,
            middle_weight,
            middle_bias,
            output_weight,
        ),
        (own_blocks, near_blocks, bond_blocks),
    )
    atom_energy = energy_blocks.reshape(domain_atoms, samples)
    forces = force_blocks.transpose(1, 0, 2, 3).reshape(3, domain_atoms, samples)
    return (atom_energy, forces)


def solution(mesh):
    return jax.shard_map(
        per_device,
        mesh=mesh,
        in_specs=(
            P("row", "col"),
            P(("col", "row"), None),
            P(None, ("col", "row"), None),
            P(("col", "row"), None),
            P(("col", "row"), None),
            P(),
            P(),
            P(),
            P(),
            P(),
        ),
        out_specs=(P(("col", "row"), None), P(None, ("col", "row"), None)),
        check_vma=False,
    )
```

profile of v0, /device:TPU:0, one launch (start us, length us, event | category | flops | bytes accessed | tf_op | source)
XLA Modules:
  0.0 321.1 jit_solution(1270470169724800918)
XLA Ops:
  8.0 44.1 %all-gather.2.cloned.1.call-done = bf16[6144,128]{1,0:T(8,128)(2,1)} async-done(((bf16[768,128]{1,0:T(8,128)(2,1)}), bf16[6144,128]{1,0:T(8,128)(2,1)}) %all-gather.2.cloned.1.call-update) | async-done | bytes 1572880 | tf_op jit(solution)/shard_map/all_gather | solution.py:82
  52.1 10.2 %fusion.22 = f32[1536,128]{1,0:T(8,128)} fusion(bf16[1536,6144]{1,0:T(8,128)(2,1)} %param.12, bf16[6144,128]{1,0:T(8,128)(2,1)} %all-gather.2.cloned.1.call-done), kind=kOutput, calls=%fused_computation.54 | convolution fusion | flops 2415919104 | bytes 21233664 | tf_op jit(solution)/shard_map/dot_general | solution.py:80
  62.6 139.8 %all-reduce.2.cloned.1.call-done = f32[1536,128]{1,0:T(8,128)} async-done(((f32[1536,128]{1,0:T(8,128)}), f32[1536,128]{1,0:T(8,128)}) %all-reduce.2.cloned.1.call-update) | async-done | bytes 786448 | tf_op jit(solution)/shard_map/psum | solution.py:88
  202.4 0.8 constant_dynamic-slice_fusion.1
  203.2 28.6 %all_gather.7 = f32[768,128]{1,0:T(8,128)S(1)} all-gather(f32[96,128]{1,0:T(8,128)S(1)} %constant_dynamic-slice_fusion.1), channel_id=1, replica_groups=mesh['row'=8,'col'=16] {'row'}, dimensions={0}, use_global_device_ids=true | all-gather | bytes 442368 | tf_op jit(solution)/shard_map/all_gather | solution.py:93
  232.6 1.0 collective-permute-start
  233.6 3.2 collective-permute-start.1
  236.9 1.7 collective-permute-done
  238.8 5.3 %collective-permute-start.3 = (f32[3,1,3,16,128]{4,2,3,1,0:T(4,128)S(1)}, f32[3,1,3,16,128]{4,2,3,1,0:T(4,128)S(1)}, u32[]{:S(2)}, u32[]{:S(2)}) collective-permute-start(f32[3,1,3,16,128]{4,2,3,1,0:T(4,128)S(1)} %pad_maximum_fusion.2), channel_id=1, source_target_pairs={{1,0},{2,1},{3,2},{4,3},{5,4},{6,5},{7,6},{8,7},{9,8},{10,9},{11,1... | collective-permute-start | bytes 221192 | tf_op jit(solution)/shard_map/ppermute | solution.py:18
  244.1 2.3 collective-permute-done.2
  246.6 2.0 gather_fusion.1
  248.9 64.7 %while.14 = (s32[]{:T(128)}, f32[4,8,128]{2,1,0:T(8,128)S(1)}, f32[4,3,8,128]{3,2,1,0:T(8,128)S(1)}, f32[4,3,8,12]{3,2,0,1:T(8,128)S(1)}, f32[4,3,8,12,128]{4,3,...) while((s32[]{:T(128)}, f32[4,8,128]{2,1,0:T(8,128)S(1)}, ...), condition=%wide.region_7.8_spmd, body=%wide.region_1.7_spmd.sunk | while | flops 1651777664 | bytes 57794740 | solution.py:116
  249.1 2.5 fusion.42
  251.5 4.5 %multiply_reduce_fusion.7 = (f32[12288]{0:T(1024)S(1)}, f32[12288,128]{1,0:T(8,128)}) fusion(f32[128]{0:T(128)S(1)} %get-tuple-element.295, f32[128]{0:T(128)S(1)} %get-tuple-element.294, bf16[128,128]{1,0:T(8,128)(2,1)S(1)} %get-tuple-element.293, f32[12288,128]{1,0:T(8,128)S(1)} %fusion.42), kind=kOutput, calls=%fused_computation.15.clone.1 | convolution fusion | flops 408932352 | bytes 12665856 | tf_op jit(solution)/shard_map/while/body/eval_jaxpr/dot_general | solution.py:49
  256.0 8.7 %fusion.43 = f32[12288]{0:T(1024)S(1)} fusion(f32[128]{0:T(128)S(1)} %iota_multiply_fusion.2, f32[12288]{0:T(1024)S(1)} %sub.114, bf16[128,128]{1,0:T(8,128)(2,1)S(1)} %get-tuple-element.291, bf16[128,128]{1,0:T(8,128)(2,1)S(1)} %get-tuple-element.293, f32[12288,128]{1,0:T(8,128)} %copy-done, f32[12288,128]{1,0:T(8,128)} %get-tuple-element.258, ...), kind=kOutput, calls=%fused_computation.23.clone.1 | convolution fusion | flops 830459904 | bytes 12747776 | tf_op jit(solution)/shard_map/while/body/eval_jaxpr/dot_general | solution.py:58
  265.2 2.5 fusion.42
  267.7 4.5 %multiply_reduce_fusion.7 = (f32[12288]{0:T(1024)S(1)}, f32[12288,128]{1,0:T(8,128)}) fusion(f32[128]{0:T(128)S(1)} %get-tuple-element.295, f32[128]{0:T(128)S(1)} %get-tuple-element.294, bf16[128,128]{1,0:T(8,128)(2,1)S(1)} %get-tuple-element.293, f32[12288,128]{1,0:T(8,128)S(1)} %fusion.42), kind=kOutput, calls=%fused_computation.15.clone.1 | convolution fusion | flops 408932352 | bytes 12665856 | tf_op jit(solution)/shard_map/while/body/eval_jaxpr/dot_general | solution.py:49
  272.2 8.7 %fusion.43 = f32[12288]{0:T(1024)S(1)} fusion(f32[128]{0:T(128)S(1)} %iota_multiply_fusion.2, f32[12288]{0:T(1024)S(1)} %sub.114, bf16[128,128]{1,0:T(8,128)(2,1)S(1)} %get-tuple-element.291, bf16[128,128]{1,0:T(8,128)(2,1)S(1)} %get-tuple-element.293, f32[12288,128]{1,0:T(8,128)} %copy-done, f32[12288,128]{1,0:T(8,128)} %get-tuple-element.258, ...), kind=kOutput, calls=%fused_computation.23.clone.1 | convolution fusion | flops 830459904 | bytes 12747776 | tf_op jit(solution)/shard_map/while/body/eval_jaxpr/dot_general | solution.py:58
  281.4 2.5 fusion.42
  283.9 4.5 %multiply_reduce_fusion.7 = (f32[12288]{0:T(1024)S(1)}, f32[12288,128]{1,0:T(8,128)}) fusion(f32[128]{0:T(128)S(1)} %get-tuple-element.295, f32[128]{0:T(128)S(1)} %get-tuple-element.294, bf16[128,128]{1,0:T(8,128)(2,1)S(1)} %get-tuple-element.293, f32[12288,128]{1,0:T(8,128)S(1)} %fusion.42), kind=kOutput, calls=%fused_computation.15.clone.1 | convolution fusion | flops 408932352 | bytes 12665856 | tf_op jit(solution)/shard_map/while/body/eval_jaxpr/dot_general | solution.py:49
  288.4 8.7 %fusion.43 = f32[12288]{0:T(1024)S(1)} fusion(f32[128]{0:T(128)S(1)} %iota_multiply_fusion.2, f32[12288]{0:T(1024)S(1)} %sub.114, bf16[128,128]{1,0:T(8,128)(2,1)S(1)} %get-tuple-element.291, bf16[128,128]{1,0:T(8,128)(2,1)S(1)} %get-tuple-element.293, f32[12288,128]{1,0:T(8,128)} %copy-done, f32[12288,128]{1,0:T(8,128)} %get-tuple-element.258, ...), kind=kOutput, calls=%fused_computation.23.clone.1 | convolution fusion | flops 830459904 | bytes 12747776 | tf_op jit(solution)/shard_map/while/body/eval_jaxpr/dot_general | solution.py:58
  297.6 2.5 fusion.42
  300.1 4.5 %multiply_reduce_fusion.7 = (f32[12288]{0:T(1024)S(1)}, f32[12288,128]{1,0:T(8,128)}) fusion(f32[128]{0:T(128)S(1)} %get-tuple-element.295, f32[128]{0:T(128)S(1)} %get-tuple-element.294, bf16[128,128]{1,0:T(8,128)(2,1)S(1)} %get-tuple-element.293, f32[12288,128]{1,0:T(8,128)S(1)} %fusion.42), kind=kOutput, calls=%fused_computation.15.clone.1 | convolution fusion | flops 408932352 | bytes 12665856 | tf_op jit(solution)/shard_map/while/body/eval_jaxpr/dot_general | solution.py:49
  304.6 8.7 %fusion.43 = f32[12288]{0:T(1024)S(1)} fusion(f32[128]{0:T(128)S(1)} %iota_multiply_fusion.2, f32[12288]{0:T(1024)S(1)} %sub.114, bf16[128,128]{1,0:T(8,128)(2,1)S(1)} %get-tuple-element.291, bf16[128,128]{1,0:T(8,128)(2,1)S(1)} %get-tuple-element.293, f32[12288,128]{1,0:T(8,128)} %copy-done, f32[12288,128]{1,0:T(8,128)} %get-tuple-element.258, ...), kind=kOutput, calls=%fused_computation.23.clone.1 | convolution fusion | flops 830459904 | bytes 12747776 | tf_op jit(solution)/shard_map/while/body/eval_jaxpr/dot_general | solution.py:58
  (98 shorter events, 4.3 us)
Async XLA Ops:
  7.2 45.0 %all-gather.2.cloned.1.call-start = ((), (), s32[]{:S(2)}) async-start(), calls=%async_computation | async-start | bytes 1769472 | tf_op jit(solution)/shard_map/all_gather | solution.py:82
  7.9 54.5 %copy-start.5 = (s32[32,12]{0,1:T(8,128)S(1)}, s32[32,12]{0,1:T(8,128)}, u32[]{:S(2)}) copy-start(s32[32,12]{0,1:T(8,128)} %param.15) | copy-start | bytes 4612
  7.9 54.7 %copy-start.8 = (s32[1,16]{1,0:T(1,128)S(1)}, s32[1,16]{1,0:T(1,128)}, u32[]{:S(2)}) copy-start(s32[1,16]{1,0:T(1,128)} %param.16) | copy-start | bytes 196
  7.9 228.9 %copy-start.2 = (f32[3,32,12]{1,2,0:T(8,128)S(1)}, f32[3,32,12]{1,2,0:T(8,128)}, u32[]{:S(2)}) copy-start(f32[3,32,12]{1,2,0:T(8,128)} %param.14) | copy-start | bytes 13828
  7.9 194.5 %all-reduce.2.cloned.1.call-start = ((), (), s32[]{:S(2)}) async-start(), calls=%async_computation.1 | async-start | bytes 1572864 | tf_op jit(solution)/shard_map/psum | solution.py:88
  62.3 186.5 %copy-start.1 = (bf16[128,128]{1,0:T(8,128)(2,1)S(1)}, bf16[128,128]{1,0:T(8,128)(2,1)}, u32[]{:S(2)}) copy-start(bf16[128,128]{1,0:T(8,128)(2,1)} %param.19) | copy-start | bytes 98308
  62.3 186.5 %copy-start.3 = (f32[128]{0:T(128)S(1)}, f32[128]{0:T(128)}, u32[]{:S(2)}) copy-start(f32[128]{0:T(128)} %param.20) | copy-start | bytes 1540
  62.3 186.5 %copy-start.4 = (f32[128]{0:T(128)S(1)}, f32[128]{0:T(128)}, u32[]{:S(2)}) copy-start(f32[128]{0:T(128)} %param.21) | copy-start | bytes 1540
  62.3 186.5 %copy-start.6 = (bf16[128,128]{1,0:T(8,128)(2,1)S(1)}, bf16[128,128]{1,0:T(8,128)(2,1)}, u32[]{:S(2)}) copy-start(bf16[128,128]{1,0:T(8,128)(2,1)} %param.17) | copy-start | bytes 98308
  62.3 186.5 %copy-start.9 = (f32[128]{0:T(128)S(1)}, f32[128]{0:T(128)}, u32[]{:S(2)}) copy-start(f32[128]{0:T(128)} %param.18) | copy-start | bytes 1540
  232.6 6.1 %collective-permute-start = (f32[1,1,3,16,128]{4,2,3,1,0:T(4,128)S(1)}, f32[1,1,3,16,128]{4,2,3,1,0:T(4,128)S(1)}, u32[]{:S(2)}, u32[]{:S(2)}) collective-permute-start(f32[1,1,3,16,128]{4,2,3,1,0:T(4,128)S(1)} %bitcast_select_fusion), channel_id=1, source_target_pairs={{0,16},{16,32},{32,48},{48,64},{64,80},{80,96},{96,112},{112,0},{1... | collective-permute-start | bytes 73736 | tf_op jit(solution)/shard_map/ppermute | solution.py:16
  233.6 5.1 %collective-permute-start.1 = (f32[1,1,3,16,128]{4,2,3,1,0:T(4,128)S(1)}, f32[1,1,3,16,128]{4,2,3,1,0:T(4,128)S(1)}, u32[]{:S(2)}, u32[]{:S(2)}) collective-permute-start(f32[1,1,3,16,128]{4,2,3,1,0:T(4,128)S(1)} %bitcast_select_fusion), channel_id=1, source_target_pairs={{16,0},{32,16},{48,32},{64,48},{80,64},{96,80},{112,96},{0,112},{1... | collective-permute-start | bytes 73736 | tf_op jit(solution)/shard_map/ppermute | solution.py:18
  238.7 7.7 %collective-permute-start.2 = (f32[3,1,3,16,128]{4,2,3,1,0:T(4,128)S(1)}, f32[3,1,3,16,128]{4,2,3,1,0:T(4,128)S(1)}, u32[]{:S(2)}, u32[]{:S(2)}) collective-permute-start(f32[3,1,3,16,128]{4,2,3,1,0:T(4,128)S(1)} %pad_maximum_fusion.2), channel_id=1, source_target_pairs={{0,1},{1,2},{2,3},{3,4},{4,5},{5,6},{6,7},{7,8},{8,9},{9,10},{10,1... | collective-permute-start | bytes 221192 | tf_op jit(solution)/shard_map/ppermute | solution.py:16
  238.8 7.6 %collective-permute-start.3 = (f32[3,1,3,16,128]{4,2,3,1,0:T(4,128)S(1)}, f32[3,1,3,16,128]{4,2,3,1,0:T(4,128)S(1)}, u32[]{:S(2)}, u32[]{:S(2)}) collective-permute-start(f32[3,1,3,16,128]{4,2,3,1,0:T(4,128)S(1)} %pad_maximum_fusion.2), channel_id=1, source_target_pairs={{1,0},{2,1},{3,2},{4,3},{5,4},{6,5},{7,6},{8,7},{9,8},{10,9},{11,1... | collective-permute-start | bytes 221192 | tf_op jit(solution)/shard_map/ppermute | solution.py:18
  251.5 4.5 %copy-start = (f32[12288,128]{1,0:T(8,128)}, f32[12288,128]{1,0:T(8,128)S(1)}, u32[]{:S(2)}) copy-start(f32[12288,128]{1,0:T(8,128)S(1)} %fusion.42) | copy-start | bytes 18874372 | tf_op jit(solution)/shard_map/while
  267.7 4.5 %copy-start = (f32[12288,128]{1,0:T(8,128)}, f32[12288,128]{1,0:T(8,128)S(1)}, u32[]{:S(2)}) copy-start(f32[12288,128]{1,0:T(8,128)S(1)} %fusion.42) | copy-start | bytes 18874372 | tf_op jit(solution)/shard_map/while
  283.9 4.5 %copy-start = (f32[12288,128]{1,0:T(8,128)}, f32[12288,128]{1,0:T(8,128)S(1)}, u32[]{:S(2)}) copy-start(f32[12288,128]{1,0:T(8,128)S(1)} %fusion.42) | copy-start | bytes 18874372 | tf_op jit(solution)/shard_map/while
  300.1 4.5 %copy-start = (f32[12288,128]{1,0:T(8,128)}, f32[12288,128]{1,0:T(8,128)S(1)}, u32[]{:S(2)}) copy-start(f32[12288,128]{1,0:T(8,128)S(1)} %fusion.42) | copy-start | bytes 18874372 | tf_op jit(solution)/shard_map/while
  313.6 0.6 copy-start.7
Sparse Core Ops, SparseCore 0:
  9.6 42.4 all-gather.1
  62.5 139.8 all-reduce.1
where the time goes:
time: 324 us; the launch traced here: 321 us
  waiting for transfers between devices  189 us (58%)
  matrix products  73.1 us (23%)
  blocking collectives  28.6 us (9%)
  between operations  14.3 us (4%)
  starting transfers between devices  9.7 us (3%)
  local copies, waits for them, and re-layouts  4.61 us (1%)
    psum x1, waiting for transfers between devices, per_device(): total = lax.psum(partial_value, 'col')  140 us
    all_gather x1, waiting for transfers between devices, per_device(): lax.all_gather(normals, 'row', axis=0, tiled=True)  44.1 us
    dot_general x4, matrix products, pair_terms(): jnp.dot(back_first, radial_weight.T, preferred_element_type=jnp.float32)  35 us
    all_gather x1, blocking collectives, per_device(): whole = lax.all_gather(slab, 'row', axis=0, tiled=True)  28.6 us
    dot_general x4, matrix products, pair_terms(): jnp.dot(first.astype(jnp.bfloat16), middle_weight, preferred_element_type...  18.1 us
    dot_general x1, matrix products, per_device(): jnp.dot(factor_panel, lax.all_gather(normals, 'row', axis=0, tiled=True),...  10.2 us
    dot_general x4, matrix products, pair_terms(): jnp.dot(flat_basis.astype(jnp.bfloat16), radial_weight, preferred_element...  9.82 us
    ppermute x2, starting transfers between devices, with_halo(): lax.ppermute(head, axis, [((i + 1) % count, i) for i in range(count)])  8.52 us
  transfers between devices with their start and end apart: 6, of which 4 were waited for; matrix products, arithmetic and copies ran while one was open for 0% of the time, Pallas kernels for 0%

commit v1 on v0

v1 whole, which is shorter than its diff:
```python
import functools
import math

import jax
import jax.numpy as jnp
from jax import lax
from jax.experimental import pallas as pl
from jax.experimental.pallas import tpu as pltpu
from jax.sharding import PartitionSpec as P

MESH = pl.DeviceIdType.MESH


def remote(src, dst, send, recv, device):
    return pltpu.make_async_remote_copy(src_ref=src, dst_ref=dst, send_sem=send, recv_sem=recv, device_id=device, device_id_type=MESH)


def displacement_kernel(sent_ref, factor_ref, normals_ref, pool_ref, fbuf, nbuf, acc, pbuf, sbuf, rbuf, disp, hsend, pool,
                        fsem, nsem, gsend, grecv, psend, precv, rsend, rrecv, tsend, trecv, hsends, hrecv, y_ready, z_ready, core_ready):
    p, q = lax.axis_index("row"), lax.axis_index("col")
    x, y_lo = lax.rem(p, 4), p // 4
    core, z, y_hi = lax.rem(q, 2), lax.rem(q // 2, 4), q // 8
    at_x = lambda step: y_lo * 4 + lax.rem(x + step, 4)
    other = lambda place: lax.rem(place + 4, 8)
    xp, xm, x2 = at_x(1), at_x(3), at_x(2)
    order = [p, xm, xp, other(p), x2, other(xm), other(xp), other(x2)]
    depth = normals_ref.shape[0]
    half = depth // 2

    own = pltpu.make_async_copy(normals_ref, nbuf.at[p], nsem)
    own.start()
    loads = []
    for k, place in enumerate(order):
        columns = pl.ds(pl.multiple_of(place * depth, depth), depth)
        loads.append(pltpu.make_async_copy(factor_ref.at[:, columns], fbuf.at[k], fsem.at[k]))
        loads[-1].start()

    x_ring = [(at_x(s), q) for s in (1, 2, 3)]
    z_ring = [(p, y_hi * 8 + lax.rem(z + s, 4) * 2 + core) for s in (1, 2, 3)]
    q_flip = lax.rem(q + 8, 16)
    y_ring = [(other(p), q), (p, q_flip), (other(p), q_flip)]
    partner = (p, q + 1 - 2 * core)
    barrier = pltpu.get_barrier_semaphore()
    for device in (*x_ring, *y_ring, *z_ring, partner):
        pl.semaphore_signal(barrier, inc=1, device_id=device, device_id_type=MESH)
    pl.semaphore_wait(barrier, 10)
    for device in y_ring:
        pl.semaphore_signal(y_ready, inc=1, device_id=device, device_id_type=MESH)

    sends = []

    def part(place, h):
        return nbuf.at[place, pl.ds(h * half, half)]

    def push(place, h, device):
        n = len(sends)
        copy = remote(part(place, h), part(place, h), gsend.at[n], grecv.at[place, h], device)
        copy.start()
        sends.append(copy)

    def arrive(place, h):
        remote(part(place, h), part(place, h), gsend.at[0], grecv.at[place, h], (p, q)).wait_recv()

    to_xp, to_xm, to_y = (xp, q), (xm, q), (other(p), q)
    own.wait()
    push(p, 0, to_xp)
    push(p, 1, to_xm)
    push(p, 0, to_y)
    push(p, 1, to_xp)
    push(p, 0, to_xm)
    push(p, 1, to_y)

    def multiply(k):
        place = order[k]
        loads[k].wait()

        def block(m, carry):
            rows = pl.ds(pl.multiple_of(m * 192, 192), 192)
            out = jnp.dot(fbuf[k, rows, :], nbuf[place], preferred_element_type=jnp.float32).reshape(2, 96, 128)
            acc[m] = out if k == 0 else acc[m] + out
            return carry

        lax.fori_loop(0, 8, block, 0)

    multiply(0)
    arrive(xm, 0)
    push(xm, 0, to_xp)
    arrive(xp, 1)
    push(xp, 1, to_xm)
    for h in (0, 1):
        arrive(other(p), h)
        push(other(p), h, to_xp)
        push(other(p), h, to_xm)
    arrive(xm, 1)
    multiply(1)
    arrive(xp, 0)
    multiply(2)
    pl.semaphore_wait(y_ready, 3)
    for device in z_ring:
        pl.semaphore_signal(z_ready, inc=1, device_id=device, device_id_type=MESH)
    arrive(x2, 0)
    push(x2, 0, to_y)
    arrive(x2, 1)
    push(x2, 1, to_y)
    multiply(3)
    multiply(4)
    pl.semaphore_wait(z_ready, 3)
    pl.semaphore_signal(core_ready, inc=1, device_id=partner, device_id_type=MESH)
    for h in (0, 1):
        arrive(other(xm), h)
    multiply(5)
    for h in (0, 1):
        arrive(other(xp), h)
    multiply(6)
    for h in (0, 1):
        arrive(other(x2), h)
    multiply(7)

    pair = remote(acc.at[:, 1 - core], pbuf, psend, precv, partner)
    pair.start()
    pl.semaphore_wait(core_ready, 1)
    pair.wait_recv()

    group = q // 2

    def spread(step, carry):
        m = lax.rem(group + step, 8)
        sbuf[m] = (acc[m, core] + pbuf[m]).reshape(6, 16, 128)
        for j in range(6):
            tile = 8 * j + p
            owner, place = tile // 6, lax.rem(tile, 6)
            remote(sbuf.at[m, j], rbuf.at[group, place], rsend.at[m], rrecv.at[group], (owner, 2 * m + core)).start()
        return carry

    lax.fori_loop(1, 8, spread, 0)
    sbuf[group] = (acc[group, core] + pbuf[group]).reshape(6, 16, 128)
    for j in range(6):
        tile = 8 * j + p
        owner, place = tile // 6, lax.rem(tile, 6)

        @pl.when(owner == p)
        def _():
            pltpu.make_async_copy(sbuf.at[group, j], rbuf.at[group, place], trecv.at[place]).start()

        @pl.when(owner != p)
        def _():
            remote(sbuf.at[group, j], rbuf.at[group, place], tsend.at[j], trecv.at[place], (owner, q)).start()

    for i in range(6):
        pltpu.make_async_copy(sbuf.at[group, 0], rbuf.at[group, i], trecv.at[i]).wait()

    def landed(step, carry):
        m = lax.rem(group + step, 8)
        remote(sbuf.at[m], rbuf.at[m], rsend.at[m], rrecv.at[m], (p, q)).wait_recv()
        return carry

    lax.fori_loop(1, 8, landed, 0)
    total = rbuf[0]
    for m in range(1, 8):
        total = total + rbuf[m]
    total = total.reshape(96, 128)
    disp[...] = total
    for c in range(3):
        pool[c, 0:32] = total[c * 32:(c + 1) * 32]
        for h in range(16):
            hsend[c, pl.ds(h, 1)] = disp[pl.ds(c * 32 + sent_ref[h], 1), :]
    halos = []
    for u in (-1, 0, 1):
        for v in (-1, 0, 1):
            slot = (u + 1) * 3 + v + 1
            if u == 0 and v == 0:
                pool[:, 32 + 16 * slot:48 + 16 * slot] = hsend[...]
                continue
            device = (lax.rem(p - u + 8, 8), lax.rem(q - v + 16, 16))
            halos.append(remote(hsend, pool.at[:, pl.ds(32 + 16 * slot, 16)], hsends.at[slot], hrecv.at[slot], device))
            halos[-1].start()
    for copy in halos:
        copy.wait_recv()
    pool_ref[...] = pool[...]
    for copy in halos:
        copy.wait_send()
    for copy in sends:
        copy.wait_send()
    pair.wait_send()

    def drained(step, carry):
        m = lax.rem(group + step, 8)
        remote(sbuf.at[m], rbuf.at[m], rsend.at[m], rrecv.at[m], (p, q)).wait_send()
        return carry

    lax.fori_loop(1, 8, drained, 0)
    for j in range(6):

        @pl.when((8 * j + p) // 6 != p)
        def _():
            remote(sbuf.at[group, j], rbuf.at[group, 0], tsend.at[j], trecv.at[0], (p, q)).wait_send()


def displacement_pool(factor_panel, normals, send_atoms):
    f32, bf16 = jnp.float32, jnp.bfloat16
    dma, regular = pltpu.SemaphoreType.DMA, pltpu.SemaphoreType.REGULAR
    rows, cols = factor_panel.shape
    depth, samples = normals.shape
    return pl.pallas_call(
        displacement_kernel,
        out_shape=jax.ShapeDtypeStruct((3, 176, samples), f32),
        in_specs=[pl.BlockSpec(memory_space=pltpu.SMEM), pl.BlockSpec(memory_space=pl.ANY), pl.BlockSpec(memory_space=pl.ANY)],
        out_specs=pl.BlockSpec(memory_space=pltpu.VMEM),
        scratch_shapes=[
            pltpu.VMEM((8, rows, depth), bf16), pltpu.VMEM((8, depth, samples), bf16),
            pltpu.VMEM((8, 2, 96, samples), f32), pltpu.VMEM((8, 96, samples), f32),
            pltpu.VMEM((8, 6, 16, samples), f32), pltpu.VMEM((8, 6, 16, samples), f32),
            pltpu.VMEM((96, samples), f32), pltpu.VMEM((3, 16, samples), f32), pltpu.VMEM((3, 176, samples), f32),
            dma((8,)), dma, dma((14,)), dma((8, 2)), dma, dma, dma((8,)), dma((8,)), dma((6,)), dma((6,)), dma((9,)), dma((9,)),
            regular, regular, regular,
        ],
        compiler_params=pltpu.CompilerParams(collective_id=0, has_side_effects=True, vmem_limit_bytes=48 * 2**20),
        name="displacements",
    )(send_atoms.reshape(-1), factor_panel, normals)


OMEGA = 90.0 / 127.0
SCALE = math.sqrt(math.log2(math.e)) / OMEGA
MU = 30.0 / 127.0


def pair_kernel(width, nb_ref, bond_ref, pool_ref, w1t_ref, w2t_ref, w2_ref, w1_ref, cols_ref,
                energy_ref, force_ref, vec_ref):
    atoms = energy_ref.shape[0]
    count = nb_ref.shape[0] // atoms
    per = width // 128

    def atom(i, carry):
        own = [pool_ref[c, pl.ds(i, 1), :] for c in range(3)]
        energy = jnp.zeros((1, 128), jnp.float32)
        force = [jnp.zeros((1, 128), jnp.float32) for _ in range(3)]
        muc = cols_ref[0]
        b1 = cols_ref[1]
        b2 = cols_ref[2]
        ow = cols_ref[3]
        if per > 1:
            muc, b1, b2, ow = [jnp.concatenate([v] * per, axis=1) for v in (muc, b1, b2, ow)]
        for g in range(count // per):
            rows = []
            vecs = []
            for h in range(per):
                n = i * count + g * per + h
                idx = nb_ref[n]
                vec = [pool_ref[c, pl.ds(idx, 1), :] + (bond_ref[c, n] - own[c]) for c in range(3)]
                vecs.append(vec)
                rows.append((vec[0] * vec[0] + vec[1] * vec[1] + vec[2] * vec[2]) * SCALE)
            sq = jnp.concatenate(rows, axis=1) if per > 1 else rows[0]
            t = sq - muc
            basis = jnp.exp2(-(t * t))
            first = jnp.tanh(jnp.dot(w1t_ref[...], basis.astype(jnp.bfloat16), preferred_element_type=jnp.float32) + b1)
            second = jnp.tanh(jnp.dot(w2t_ref[...], first.astype(jnp.bfloat16), preferred_element_type=jnp.float32) + b2)
            so = second * ow
            phi = jnp.sum(so, axis=0, keepdims=True)
            back2 = (ow - second * so).astype(jnp.bfloat16)
            back1 = (jnp.dot(w2_ref[...], back2, preferred_element_type=jnp.float32) * (1.0 - first * first)).astype(jnp.bfloat16)
            grad = jnp.dot(w1_ref[...], back1, preferred_element_type=jnp.float32)
            slope = jnp.sum(grad * (basis * t), axis=0, keepdims=True)
            for h in range(per):
                energy = energy + phi[:, h * 128:(h + 1) * 128]
                for c in range(3):
                    force[c] = force[c] + slope[:, h * 128:(h + 1) * 128] * vecs[h][c]
        energy_ref[pl.ds(i, 1), :] = 0.5 * energy
        for c in range(3):
            force_ref[c, pl.ds(i, 1), :] = force[c] * (2.0 * -2.0 / (OMEGA * OMEGA * SCALE))
        return carry

    lax.fori_loop(0, atoms, atom, 0)


def pair_stage(pool, bond, nb, w1, b1, w2, b2, ow, width=1536):
    atoms = bond.shape[1]
    samples = pool.shape[2]
    cols = jnp.stack([jnp.arange(128, dtype=jnp.float32) * (MU * SCALE), b1, b2, ow])
    cols = jnp.broadcast_to(cols[:, :, None], (4, 128, 128))
    V = pl.BlockSpec(memory_space=pltpu.VMEM)
    S = pl.BlockSpec(memory_space=pltpu.SMEM)
    return pl.pallas_call(
        functools.partial(pair_kernel, width),
        out_shape=(jax.ShapeDtypeStruct((atoms, samples), jnp.float32), jax.ShapeDtypeStruct((3, atoms, samples), jnp.float32)),
        in_specs=[S, S, V, V, V, V, V, V],
        out_specs=(V, V),
        scratch_shapes=[pltpu.VMEM((3, 384, 128), jnp.float32)],
        name="pairs",
    )(nb.reshape(-1), bond.reshape(3, -1), pool, w1.T, w2.T, w2, w1, cols)


def per_device(factor_panel, normals, bond_vectors, neighbours, send_atoms, radial_weight, radial_bias, middle_weight, middle_bias, output_weight):
    pool = displacement_pool(factor_panel, normals, send_atoms)
    return pair_stage(pool, bond_vectors, neighbours, radial_weight, radial_bias, middle_weight, middle_bias, output_weight)


def solution(mesh):
    whole = P(("col", "row"), None)
    return jax.shard_map(
        per_device,
        mesh=mesh,
        in_specs=(P("row", "col"), whole, P(None, ("col", "row"), None), whole, whole, P(), P(), P(), P(), P()),
        out_specs=(whole, P(None, ("col", "row"), None)),
        check_vma=False,
    )
```

time: 324 us -> 88.7 us (0.27)
  waiting for transfers between devices: 189 us -> 0 us
  Pallas kernels: 0 us -> 77.9 us
  matrix products: 73.1 us -> 0 us
  blocking collectives: 28.6 us -> 0 us
  between operations: 14.3 us -> 0.66 us
  starting transfers between devices: 9.7 us -> 0 us
  local copies, waits for them, and re-layouts: 4.61 us -> 8.98 us
    psum x1 -> x0, waiting for transfers between devices: 140 us -> none  [per_device(): total = lax.psum(partial_value, 'col')]
    pallas_call x0 -> x2, Pallas kernels: none -> 77.9 us  [the longest x1 43.6 us: displacement_pool(): pl.pallas_call(displacement_kernel, out_shape=jax.ShapeDtypeStruct((3, 17...]
    dot_general x13 -> x0, matrix products: 73.1 us -> none  [the longest x4 35 us: pair_terms(): jnp.dot(back_first, radial_weight.T, preferred_element_type=jnp.float32)]
    all_gather x1 -> x0, waiting for transfers between devices: 44.1 us -> none  [per_device(): lax.all_gather(normals, 'row', axis=0, tiled=True)]
    all_gather x1 -> x0, blocking collectives: 28.6 us -> none  [per_device(): whole = lax.all_gather(slab, 'row', axis=0, tiled=True)]
    ppermute x4 -> x0, starting transfers between devices: 9.63 us -> none  [the longest x2 8.52 us: with_halo(): lax.ppermute(head, axis, [((i + 1) % count, i) for i in range(count)])]
    unnamed x20 -> x10, local copies, waits for them, and re-layouts: 0.23 us -> 6.78 us
    ppermute x4 -> x0, waiting for transfers between devices: 4.04 us -> none  [the longest x2 4.03 us: with_halo(): lax.ppermute(tail, axis, [(i, (i + 1) % count) for i in range(count)])]
  transfers between devices with their start and end apart: 6 -> 0, of which waited for: 4 -> 0; matrix products, arithmetic and copies ran while one was open for 0% -> 0% of each run, Pallas kernels for 0% -> 0%
where the time goes in v1:
time: 88.7 us; the launch traced here: 88.2 us
  Pallas kernels  77.9 us (88%)
  local copies, waits for them, and re-layouts  8.98 us (10%)
    pallas_call x1, Pallas kernels, displacement_pool(): pl.pallas_call(displacement_kernel, out_shape=jax.ShapeDtypeStruct((3, 17...  43.6 us
    pallas_call x1, Pallas kernels, pair_stage(): pl.pallas_call(functools.partial(pair_kernel, width), out_shape=(jax.Shap...  34.3 us
    unnamed x10, local copies, waits for them, and re-layouts  6.78 us

profile of v1, /device:TPU:0, one launch (start us, length us, event | category | flops | bytes accessed | tf_op | source)
XLA Modules:
  0.0 88.2 jit_solution(4699381313563971581)
XLA Ops:
  0.6 0.7 pad_maximum_fusion
  1.3 0.8 copy.15
  2.1 0.7 reshape.21.nb_ref
  2.8 1.5 %copy.17 = bf16[128,128]{0,1:T(8,128)(2,1)} copy(bf16[128,128]{1,0:T(8,128)(2,1)} %w1_ref.1) | data formatting | bytes 65536 | tf_op args[5]
  4.3 1.5 %copy.18 = bf16[128,128]{0,1:T(8,128)(2,1)} copy(bf16[128,128]{1,0:T(8,128)(2,1)} %w2_ref.1) | data formatting | bytes 65536 | tf_op args[7]
  5.7 0.8 copy.16
  6.6 0.7 reshape.22.bond_ref
  7.2 0.8 broadcast_in_dim.2.cols_ref
  8.1 0.0 copy-start.1
  8.1 0.9 %copy-done.1 = bf16[768,128]{1,0:T(8,128)(2,1)S(1)} copy-done((bf16[768,128]{1,0:T(8,128)(2,1)S(1)}, bf16[768,128]{1,0:T(8,128)(2,1)}, u32[]{:S(2)}) %copy-start.1) | copy-done | bytes 196632
  9.0 0.0 copy-start.2
  9.0 0.7 copy-done.2
  9.6 43.6 %displacements.1.pool_ref = f32[3,176,128]{2,1,0:T(8,128)S(1)} custom-call(s32[16]{0:T(128)S(1)} %bitcast.6, bf16[1536,6144]{1,0:T(8,128)(2,1)} %factor_ref.1, bf16[768,128]{1,0:T(8,128)(2,1)S(1)} %copy-done.1), custom_call_target="tpu_custom_call" | custom-call | tf_op jit(solution)/shard_map/displacements/pallas_call | solution.py:204
  53.2 0.0 copy-start
  53.2 0.7 copy-done
  53.9 34.3 %pairs.1 = (f32[32,128]{1,0:T(8,128)}, f32[3,32,128]{2,1,0:T(8,128)}) custom-call(s32[384]{0:T(512)} %reshape.21.nb_ref, f32[3,384]{1,0:T(4,128)} %reshape.22.bond_ref, f32[3,176,128]{2,1,0:T(8,128)} %copy-done, bf16[128,128]{1,0:T(8,128)(2,1)} %bitcast.7, bf16[128,128]{1,0:T(8,128)(2,1)} %bitcast.8, bf16[128,128]{1,0:T(8,128)(2,1)} %w2_ref.1, ...), custom_call_target="tpu_custom_call" | custom-call | tf_op jit(solution)/shard_map/pairs/pallas_call | solution.py:282
  (1 shorter events, 0.0 us)
Async XLA Ops:
  8.1 0.9 %copy-start.1 = (bf16[768,128]{1,0:T(8,128)(2,1)S(1)}, bf16[768,128]{1,0:T(8,128)(2,1)}, u32[]{:S(2)}) copy-start(bf16[768,128]{1,0:T(8,128)(2,1)} %normals_ref.1) | copy-start | bytes 589828
  9.0 0.7 copy-start.2
  53.2 0.7 copy-start

commit v2 on v1

v2 whole, which is shorter than its diff:
```python
import functools
import math

import jax
import jax.numpy as jnp
from jax import lax
from jax.experimental import pallas as pl
from jax.experimental.pallas import tpu as pltpu
from jax.sharding import PartitionSpec as P

MESH = pl.DeviceIdType.MESH


def remote(src, dst, send, recv, device):
    return pltpu.make_async_remote_copy(src_ref=src, dst_ref=dst, send_sem=send, recv_sem=recv, device_id=device, device_id_type=MESH)


def displacement_kernel(sent_hbm, factor_ref, normals_ref, pool_ref, fbuf, nbuf, acc, pbuf, sbuf, rbuf, disp, hsend, pool,
                        fsem, nsem, gsend, grecv, psend, precv, rsend, rrecv, tsend, trecv, hsends, hrecv, y_ready, z_ready, core_ready, sent_ref, sent_sem):
    p, q = lax.axis_index("row"), lax.axis_index("col")
    x, y_lo = lax.rem(p, 4), p // 4
    core, z, y_hi = lax.rem(q, 2), lax.rem(q // 2, 4), q // 8
    at_x = lambda step: y_lo * 4 + lax.rem(x + step, 4)
    other = lambda place: lax.rem(place + 4, 8)
    xp, xm, x2 = at_x(1), at_x(3), at_x(2)
    order = [p, xm, xp, other(p), x2, other(xm), other(xp), other(x2)]
    depth = normals_ref.shape[0]
    half = depth // 2

    own = pltpu.make_async_copy(normals_ref, nbuf.at[p], nsem)
    own.start()
    sent_in = pltpu.make_async_copy(sent_hbm, sent_ref, sent_sem)
    sent_in.start()
    loads = []
    for k, place in enumerate(order):
        columns = pl.ds(pl.multiple_of(place * depth, depth), depth)
        loads.append([pltpu.make_async_copy(factor_ref.at[:, side, :, columns], fbuf.at[k, part], fsem.at[k, part])
                      for part, side in enumerate((1 - core, core))])
        for copy in loads[-1]:
            copy.start()

    x_ring = [(at_x(s), q) for s in (1, 2, 3)]
    z_ring = [(p, y_hi * 8 + lax.rem(z + s, 4) * 2 + core) for s in (1, 2, 3)]
    q_flip = lax.rem(q + 8, 16)
    y_ring = [(other(p), q), (p, q_flip), (other(p), q_flip)]
    partner = (p, q + 1 - 2 * core)
    barrier = pltpu.get_barrier_semaphore()
    for device in (*x_ring, *y_ring, *z_ring, partner):
        pl.semaphore_signal(barrier, inc=1, device_id=device, device_id_type=MESH)
    pl.semaphore_wait(barrier, 10)
    for device in y_ring:
        pl.semaphore_signal(y_ready, inc=1, device_id=device, device_id_type=MESH)

    sends = []

    def part(place, h):
        return nbuf.at[place, pl.ds(h * half, half)]

    def push(place, h, device):
        n = len(sends)
        copy = remote(part(place, h), part(place, h), gsend.at[n], grecv.at[place, h], device)
        copy.start()
        sends.append(copy)

    def arrive(place, h):
        remote(part(place, h), part(place, h), gsend.at[0], grecv.at[place, h], (p, q)).wait_recv()

    to_xp, to_xm, to_y = (xp, q), (xm, q), (other(p), q)
    own.wait()
    push(p, 0, to_xp)
    push(p, 1, to_xm)
    push(p, 0, to_y)
    push(p, 1, to_xp)
    push(p, 0, to_xm)
    push(p, 1, to_y)

    def product(k, part):
        weights = nbuf[order[k]]
        out = jnp.dot(fbuf[k, part].reshape(768, depth), weights, preferred_element_type=jnp.float32).reshape(8, 96, 128)
        acc[part] = out if k == 0 else acc[part] + out

    def multiply(k):
        for copy in loads[k]:
            copy.wait()

        def half_rows(part, carry):
            product(k, part)
            return carry

        lax.fori_loop(0, 2, half_rows, 0)

    multiply(0)
    arrive(xm, 0)
    push(xm, 0, to_xp)
    arrive(xp, 1)
    push(xp, 1, to_xm)
    for h in (0, 1):
        arrive(other(p), h)
        push(other(p), h, to_xp)
        push(other(p), h, to_xm)
    arrive(xm, 1)
    multiply(1)
    arrive(xp, 0)
    multiply(2)
    pl.semaphore_wait(y_ready, 3)
    for device in z_ring:
        pl.semaphore_signal(z_ready, inc=1, device_id=device, device_id_type=MESH)
    arrive(x2, 0)
    push(x2, 0, to_y)
    arrive(x2, 1)
    push(x2, 1, to_y)
    multiply(3)
    multiply(4)
    pl.semaphore_wait(z_ready, 3)
    pl.semaphore_signal(core_ready, inc=1, device_id=partner, device_id_type=MESH)
    for h in (0, 1):
        arrive(other(xm), h)
    multiply(5)
    for h in (0, 1):
        arrive(other(xp), h)
    multiply(6)
    for h in (0, 1):
        arrive(other(x2), h)
    for copy in loads[7]:
        copy.wait()
    group = q // 2

    def ahead(step):
        late = step // 4
        shift = (1 - late) * lax.rem(2 + step, 4) + late * (1 + lax.rem(step, 3))
        return lax.rem(y_hi + 1 - late, 2) * 4 + lax.rem(z + shift, 4)

    def swap(m):
        return remote(acc.at[0, m], pbuf.at[m], psend.at[m], precv.at[m], partner)

    product(7, 0)

    def swap_out(step, carry):
        swap(ahead(step)).start()
        return carry

    lax.fori_loop(0, 7, swap_out, 0)
    swap(group).start()
    product(7, 1)
    pl.semaphore_wait(core_ready, 1)

    def spread(step, carry):
        m = ahead(step)
        swap(m).wait_recv()
        sbuf[m] = (acc[1, m] + pbuf[m]).reshape(6, 16, 128)
        for j in range(6):
            tile = 8 * j + p
            owner, place = tile // 6, lax.rem(tile, 6)
            remote(sbuf.at[m, j], rbuf.at[group, place], rsend.at[m], rrecv.at[group], (owner, 2 * m + core)).start()
        return carry

    lax.fori_loop(0, 7, spread, 0)
    swap(group).wait_recv()
    sbuf[group] = (acc[1, group] + pbuf[group]).reshape(6, 16, 128)
    for j in range(6):
        tile = 8 * j + p
        owner, place = tile // 6, lax.rem(tile, 6)

        @pl.when(owner == p)
        def _():
            pltpu.make_async_copy(sbuf.at[group, j], rbuf.at[group, place], trecv.at[place]).start()

        @pl.when(owner != p)
        def _():
            remote(sbuf.at[group, j], rbuf.at[group, place], tsend.at[j], trecv.at[place], (owner, q)).start()

    for i in range(6):
        pltpu.make_async_copy(sbuf.at[group, 0], rbuf.at[group, i], trecv.at[i]).wait()

    def landed(step, carry):
        m = lax.rem(group + step, 8)
        remote(sbuf.at[m], rbuf.at[m], rsend.at[m], rrecv.at[m], (p, q)).wait_recv()
        return carry

    lax.fori_loop(1, 8, landed, 0)
    sent_in.wait()
    total = rbuf[0]
    for m in range(1, 8):
        total = total + rbuf[m]
    total = total.reshape(96, 128)
    disp[...] = total
    for c in range(3):
        pool[c, 0:32] = total[c * 32:(c + 1) * 32]
        for h in range(16):
            hsend[c, pl.ds(h, 1)] = disp[pl.ds(c * 32 + sent_ref[0, h], 1), :]
    halos = []
    for u in (-1, 0, 1):
        for v in (-1, 0, 1):
            slot = (u + 1) * 3 + v + 1
            if u == 0 and v == 0:
                pool[:, 32 + 16 * slot:48 + 16 * slot] = hsend[...]
                continue
            device = (lax.rem(p - u + 8, 8), lax.rem(q - v + 16, 16))
            halos.append(remote(hsend, pool.at[:, pl.ds(32 + 16 * slot, 16)], hsends.at[slot], hrecv.at[slot], device))
            halos[-1].start()
    for copy in halos:
        copy.wait_recv()
    pool_ref[...] = pool[...]
    for copy in halos:
        copy.wait_send()
    for copy in sends:
        copy.wait_send()
    for m in range(8):
        swap(m).wait_send()

    def drained(step, carry):
        m = lax.rem(group + step, 8)
        remote(sbuf.at[m], rbuf.at[m], rsend.at[m], rrecv.at[m], (p, q)).wait_send()
        return carry

    lax.fori_loop(1, 8, drained, 0)
    for j in range(6):

        @pl.when((8 * j + p) // 6 != p)
        def _():
            remote(sbuf.at[group, j], rbuf.at[group, 0], tsend.at[j], trecv.at[0], (p, q)).wait_send()


def displacement_pool(factor_panel, normals, send_atoms):
    f32, bf16 = jnp.float32, jnp.bfloat16
    dma, regular = pltpu.SemaphoreType.DMA, pltpu.SemaphoreType.REGULAR
    rows, cols = factor_panel.shape
    depth, samples = normals.shape
    return pl.pallas_call(
        displacement_kernel,
        out_shape=jax.ShapeDtypeStruct((3, 176, samples), f32),
        in_specs=[pl.BlockSpec(memory_space=pltpu.HBM), pl.BlockSpec(memory_space=pltpu.HBM), pl.BlockSpec(memory_space=pltpu.HBM)],
        out_specs=pl.BlockSpec(memory_space=pltpu.VMEM),
        scratch_shapes=[
            pltpu.VMEM((8, 2, 8, 96, depth), bf16), pltpu.VMEM((8, depth, samples), bf16),
            pltpu.VMEM((2, 8, 96, samples), f32), pltpu.VMEM((8, 96, samples), f32),
            pltpu.VMEM((8, 6, 16, samples), f32), pltpu.VMEM((8, 6, 16, samples), f32),
            pltpu.VMEM((96, samples), f32), pltpu.VMEM((3, 16, samples), f32), pltpu.VMEM((3, 176, samples), f32),
            dma((8, 2)), dma, dma((14,)), dma((8, 2)), dma((8,)), dma((8,)), dma((8,)), dma((8,)), dma((6,)), dma((6,)), dma((9,)), dma((9,)),
            regular, regular, regular, pltpu.SMEM((1, 16), jnp.int32), dma,
        ],
        compiler_params=pltpu.CompilerParams(collective_id=0, has_side_effects=True, vmem_limit_bytes=48 * 2**20),
        name="displacements",
    )(pltpu.with_memory_space_constraint(send_atoms, pltpu.HBM), factor_panel.reshape(8, 2, 96, cols), pltpu.with_memory_space_constraint(normals, pltpu.HBM))


OMEGA = 90.0 / 127.0
SCALE = math.sqrt(math.log2(math.e)) / OMEGA
MU = 30.0 / 127.0


def pieces(column):
    high = column.astype(jnp.bfloat16)
    rest = column - high.astype(jnp.float32)
    middle = rest.astype(jnp.bfloat16)
    low = (rest - middle.astype(jnp.float32)).astype(jnp.bfloat16)
    return high, middle, low


def beside(weights_t, bias):
    place = lax.broadcasted_iota(jnp.int32, (128, 128), 1)
    high, middle, low = [v.astype(jnp.float32) for v in pieces(bias)]
    extra = jnp.where(place == 0, high, jnp.where(place == 1, middle, jnp.where(place == 2, low, 0.0)))
    return jnp.concatenate([weights_t, extra.astype(jnp.bfloat16)], axis=1)[:, :144]


def pair_kernel(group, split, offset, nb_ref, bond_ref, pool_ref, w1_ref, b1_ref, w2_ref, b2_ref, ow_ref,
                energy_ref, force_ref, muc_ref, ow_s, w1a, w2a):
    atoms = energy_ref.shape[0]
    count = nb_ref.shape[0]
    bf16, f32 = jnp.bfloat16, jnp.float32
    spread = lambda ref: jnp.broadcast_to(ref[...].reshape(1, 128), (128, 128))
    muc_ref[...] = lax.broadcasted_iota(jnp.int32, (128, 128), 0).astype(f32) * (MU * SCALE)
    ow_s[...] = spread(ow_ref).T
    w1a[...] = beside(w1_ref[...].T, spread(b1_ref).T)
    w2a[...] = beside(w2_ref[...].T, spread(b2_ref).T)
    wide = count * 128
    tile = lambda v: jnp.concatenate([v] * (wide // 128), axis=1)
    dot = functools.partial(jnp.dot, preferred_element_type=f32)
    ones = jnp.where(lax.broadcasted_iota(jnp.int32, (16, wide), 0) < 3, 1.0, 0.0).astype(bf16)
    dense = lambda w, v: dot(w[...], jnp.concatenate([v.astype(bf16), ones], axis=0))

    def work(i, pairs):
        own = [pool_ref[c, pl.ds(i, 1), :] for c in range(3)]
        rows, vecs = [], []
        for n in pairs:
            idx = nb_ref[n, i]
            vec = [pool_ref[c, pl.ds(idx, 1), :] + (bond_ref[c, n, i] - own[c]) for c in range(3)]
            vecs.append(vec)
            rows.append((vec[0] * vec[0] + vec[1] * vec[1] + vec[2] * vec[2]) * SCALE)
        tile = lambda v: jnp.concatenate([v] * len(pairs), axis=1)
        ones = jnp.where(lax.broadcasted_iota(jnp.int32, (16, 128 * len(pairs)), 0) < 3, 1.0, 0.0).astype(bf16)
        dense = lambda w, v: dot(w[...], jnp.concatenate([v.astype(bf16), ones], axis=0))
        t = jnp.concatenate(rows, axis=1) - tile(muc_ref[...])
        yield
        basis = jnp.exp2(-(t * t))
        yield
        bt = basis * t
        z1 = dense(w1a, basis)
        yield
        first = jnp.tanh(z1)
        yield
        z2 = dense(w2a, first)
        yield
        second = jnp.tanh(z2)
        yield
        ow = tile(ow_s[...])
        so = second * ow
        back2 = (ow - second * so).astype(bf16)
        phi = jnp.sum(so, axis=0, keepdims=True)
        yield
        back1 = (dot(w2_ref[...], back2) * (1.0 - first * first)).astype(bf16)
        yield
        slope = jnp.sum(dot(w1_ref[...], back1) * bt, axis=0, keepdims=True)
        at = lambda v, n: v[:, n * 128:(n + 1) * 128]
        energy = sum(at(phi, n) for n in range(len(pairs)))
        force = [sum(at(slope, n) * vecs[n][c] for n in range(len(pairs))) for c in range(3)]
        sums[i_key(i)].append((energy, force))
        yield

    sums = {}
    keys = []

    def i_key(i):
        return [k for k, v in keys if v is i][0]

    def run(items, offset):
        gens = [work(i, p) for i, p in items]
        for step in range(9 + offset * (len(gens) - 1)):
            for g, gen in enumerate(gens):
                if 0 <= step - offset * g < 9:
                    next(gen)

    def body(k, carry):
        sums.clear()
        keys.clear()
        items = []
        for a in range(group):
            i = k * group + a
            keys.append((a, i))
            sums[a] = []
            per = count // split
            for h in range(split):
                items.append((i, range(h * per, (h + 1) * per)))
        run(items, offset)
        for a, i in keys:
            energy = sum(v[0] for v in sums[a])
            energy_ref[pl.ds(i, 1), :] = 0.5 * energy
            for c in range(3):
                force_ref[c, pl.ds(i, 1), :] = sum(v[1][c] for v in sums[a]) * (-4.0 / (OMEGA * OMEGA * SCALE))
        return carry

    lax.fori_loop(0, atoms // group, body, 0)


def pair_stage(pool, bond, nb, w1, b1, w2, b2, ow, group=2, split=1, offset=0):
    atoms = bond.shape[1]
    samples = pool.shape[2]
    V = pl.BlockSpec(memory_space=pltpu.VMEM)
    S = pl.BlockSpec(memory_space=pltpu.SMEM)
    f32, bf16 = jnp.float32, jnp.bfloat16
    return pl.pallas_call(
        functools.partial(pair_kernel, group, split, offset),
        out_shape=(jax.ShapeDtypeStruct((atoms, samples), f32), jax.ShapeDtypeStruct((3, atoms, samples), f32)),
        in_specs=[S, S, V, V, V, V, V, V],
        out_specs=(V, V),
        scratch_shapes=[pltpu.VMEM((128, 128), f32)] * 2 + [pltpu.VMEM((128, 144), bf16)] * 2,
        compiler_params=pltpu.CompilerParams(vmem_limit_bytes=16 * 2**20),
        name="pairs",
    )(nb.T, bond.transpose(0, 2, 1), pool, w1, b1, w2, b2, ow)


def per_device(factor_panel, normals, bond_vectors, neighbours, send_atoms, radial_weight, radial_bias, middle_weight, middle_bias, output_weight):
    pool = displacement_pool(factor_panel, normals, send_atoms)
    return pair_stage(pool, bond_vectors, neighbours, radial_weight, radial_bias, middle_weight, middle_bias, output_weight)


def solution(mesh):
    whole = P(("col", "row"), None)
    return jax.shard_map(
        per_device,
        mesh=mesh,
        in_specs=(P("row", "col"), whole, P(None, ("col", "row"), None), whole, whole, P(), P(), P(), P(), P()),
        out_specs=(whole, P(None, ("col", "row"), None)),
        check_vma=False,
    )
```

time: 88.7 us -> 65 us (0.73)
  Pallas kernels: 77.9 us -> 63.4 us
  local copies, waits for them, and re-layouts: 8.98 us -> 0.03 us
    pallas_call x1, Pallas kernels: 34.3 us -> 25.8 us  [pair_stage(): pl.pallas_call(functools.partial(pair_kernel, group, split, offset), out_...]
    unnamed x10 -> x14, local copies, waits for them, and re-layouts: 6.78 us -> 0.03 us
    pallas_call x1, Pallas kernels: 43.6 us -> 37.5 us  [displacement_pool(): pl.pallas_call(displacement_kernel, out_shape=jax.ShapeDtypeStruct((3, 17...]
    reshape x2 -> x0, local copies, waits for them, and re-layouts: 1.37 us -> none  [the longest x1 0.69 us: pair_stage(): nb.reshape(-1)]
where the time goes in v2:
time: 65 us; the launch traced here: 64.2 us
  Pallas kernels  63.4 us (98%)
  between operations  0.75 us (1%)
    pallas_call x1, Pallas kernels, displacement_pool(): pl.pallas_call(displacement_kernel, out_shape=jax.ShapeDtypeStruct((3, 17...  37.5 us
    pallas_call x1, Pallas kernels, pair_stage(): pl.pallas_call(functools.partial(pair_kernel, group, split, offset), out_...  25.8 us

profile of v2, /device:TPU:0, one launch (start us, length us, event | category | flops | bytes accessed | tf_op | source)
XLA Modules:
  0.0 64.2 jit_solution(17254773792241332823)
XLA Ops:
  0.6 0.0 copy-start.6
  0.6 0.0 copy-start.5
  0.7 0.0 copy-start.1
  0.7 0.0 copy-start.4
  0.7 0.0 copy-start
  0.7 0.0 copy-start.3
  0.7 0.0 copy-start.2
  0.7 37.5 %displacements.1.pool_ref = f32[3,176,128]{2,1,0:T(8,128)S(1)} custom-call(s32[1,16]{1,0:T(1,128)} %sent_hbm.1, bf16[8,2,96,6144]{3,2,1,0:T(8,128)(2,1)} %bitcast.5, bf16[768,128]{1,0:T(8,128)(2,1)} %normals_ref.1), custom_call_target="tpu_custom_call" | custom-call | tf_op jit(solution)/shard_map/displacements/pallas_call | solution.py:229
  38.2 0.0 copy-done.6
  38.3 0.0 copy-done.5
  38.3 0.0 copy-done.1
  38.3 0.0 copy-done.4
  38.3 0.0 copy-done
  38.3 0.0 copy-done.3
  38.3 0.0 copy-done.2
  38.3 25.8 %pairs.1 = (f32[32,128]{1,0:T(8,128)}, f32[3,32,128]{2,1,0:T(8,128)}) custom-call(s32[12,32]{1,0:T(8,128)S(1)} %bitcast.4, f32[3,12,32]{2,1,0:T(8,128)S(1)} %bitcast.3, f32[3,176,128]{2,1,0:T(8,128)S(1)} %displacements.1.pool_ref, bf16[128,128]{1,0:T(8,128)(2,1)S(1)} %copy-done, f32[128]{0:T(128)S(1)} %copy-done.4, bf16[128,128]{1,0:T(8,128)(2,1)S(1)} %copy-done.1, ...), custom_call_target="tpu_custom_call" | custom-call | tf_op jit(solution)/shard_map/pairs/pallas_call | solution.py:362
Async XLA Ops:
  0.6 37.6 %copy-start.6 = (f32[128]{0:T(128)S(1)}, f32[128]{0:T(128)}, u32[]{:S(2)}) copy-start(f32[128]{0:T(128)} %ow_ref.1) | copy-start | bytes 1540
  0.6 37.6 %copy-start.5 = (f32[128]{0:T(128)S(1)}, f32[128]{0:T(128)}, u32[]{:S(2)}) copy-start(f32[128]{0:T(128)} %b2_ref.1) | copy-start | bytes 1540
  0.7 37.6 %copy-start.1 = (bf16[128,128]{1,0:T(8,128)(2,1)S(1)}, bf16[128,128]{1,0:T(8,128)(2,1)}, u32[]{:S(2)}) copy-start(bf16[128,128]{1,0:T(8,128)(2,1)} %w2_ref.1) | copy-start | bytes 98308
  0.7 37.6 %copy-start.4 = (f32[128]{0:T(128)S(1)}, f32[128]{0:T(128)}, u32[]{:S(2)}) copy-start(f32[128]{0:T(128)} %b1_ref.1) | copy-start | bytes 1540
  0.7 37.6 %copy-start = (bf16[128,128]{1,0:T(8,128)(2,1)S(1)}, bf16[128,128]{1,0:T(8,128)(2,1)}, u32[]{:S(2)}) copy-start(bf16[128,128]{1,0:T(8,128)(2,1)} %w1_ref.1) | copy-start | bytes 98308
  0.7 37.6 %copy-start.3 = (s32[32,12]{0,1:T(8,128)S(1)}, s32[32,12]{0,1:T(8,128)}, u32[]{:S(2)}) copy-start(s32[32,12]{0,1:T(8,128)} %param.13) | copy-start | bytes 4612
  0.7 37.6 %copy-start.2 = (f32[3,32,12]{1,2,0:T(8,128)S(1)}, f32[3,32,12]{1,2,0:T(8,128)}, u32[]{:S(2)}) copy-start(f32[3,32,12]{1,2,0:T(8,128)} %param.12) | copy-start | bytes 13828

commit v3 on v2

--- a/solution.py
+++ b/solution.py
@@ -264,107 +264,70 @@
     return jnp.concatenate([weights_t, extra.astype(jnp.bfloat16)], axis=1)[:, :144]
 
 
-def pair_kernel(group, split, offset, nb_ref, bond_ref, pool_ref, w1_ref, b1_ref, w2_ref, b2_ref, ow_ref,
-                energy_ref, force_ref, muc_ref, ow_s, w1a, w2a):
+def pair_kernel(group, nb_ref, bond_ref, pool_ref, w1_ref, b1_ref, w2_ref, b2_ref, ow_ref,
+                energy_ref, force_ref, muc_ref, w1a, w2a, w2o):
     atoms = energy_ref.shape[0]
     count = nb_ref.shape[0]
     bf16, f32 = jnp.bfloat16, jnp.float32
     spread = lambda ref: jnp.broadcast_to(ref[...].reshape(1, 128), (128, 128))
     muc_ref[...] = lax.broadcasted_iota(jnp.int32, (128, 128), 0).astype(f32) * (MU * SCALE)
-    ow_s[...] = spread(ow_ref).T
     w1a[...] = beside(w1_ref[...].T, spread(b1_ref).T)
     w2a[...] = beside(w2_ref[...].T, spread(b2_ref).T)
-    wide = count * 128
-    tile = lambda v: jnp.concatenate([v] * (wide // 128), axis=1)
+    scaled = (w2_ref[...].astype(f32) * spread(ow_ref)).astype(bf16)
+    line = lax.broadcasted_iota(jnp.int32, (16, 128), 0)
+    high, middle, low = [v.astype(f32)[:16] for v in pieces(spread(ow_ref))]
+    read = jnp.where(line == 0, high, jnp.where(line == 1, middle, jnp.where(line == 2, low, 0.0))).astype(bf16)
+    w2o[...] = jnp.concatenate([
+        jnp.concatenate([scaled, jnp.zeros((128, 128), bf16)], axis=1),
+        jnp.concatenate([jnp.zeros((16, 128), bf16), read], axis=1)], axis=0)
     dot = functools.partial(jnp.dot, preferred_element_type=f32)
+    wide = group * count * 128
     ones = jnp.where(lax.broadcasted_iota(jnp.int32, (16, wide), 0) < 3, 1.0, 0.0).astype(bf16)
-    dense = lambda w, v: dot(w[...], jnp.concatenate([v.astype(bf16), ones], axis=0))
-
-    def work(i, pairs):
-        own = [pool_ref[c, pl.ds(i, 1), :] for c in range(3)]
+    at = lambda v, n: v[:, n * 128:(n + 1) * 128]
+
+    def body(k, carry):
         rows, vecs = [], []
-        for n in pairs:
-            idx = nb_ref[n, i]
-            vec = [pool_ref[c, pl.ds(idx, 1), :] + (bond_ref[c, n, i] - own[c]) for c in range(3)]
-            vecs.append(vec)
-            rows.append((vec[0] * vec[0] + vec[1] * vec[1] + vec[2] * vec[2]) * SCALE)
-        tile = lambda v: jnp.concatenate([v] * len(pairs), axis=1)
-        ones = jnp.where(lax.broadcasted_iota(jnp.int32, (16, 128 * len(pairs)), 0) < 3, 1.0, 0.0).astype(bf16)
-        dense = lambda w, v: dot(w[...], jnp.concatenate([v.astype(bf16), ones], axis=0))
-        t = jnp.concatenate(rows, axis=1) - tile(muc_ref[...])
-        yield
-        basis = jnp.exp2(-(t * t))
-        yield
-        bt = basis * t
-        z1 = dense(w1a, basis)
-        yield
-        first = jnp.tanh(z1)
-        yield
-        z2 = dense(w2a, first)
-        yield
-        second = jnp.tanh(z2)
-        yield
-        ow = tile(ow_s[...])
-        so = second * ow
-        back2 = (ow - second * so).astype(bf16)
-        phi = jnp.sum(so, axis=0, keepdims=True)
-        yield
-        back1 = (dot(w2_ref[...], back2) * (1.0 - first * first)).astype(bf16)
-        yield
-        slope = jnp.sum(dot(w1_ref[...], back1) * bt, axis=0, keepdims=True)
-        at = lambda v, n: v[:, n * 128:(n + 1) * 128]
-        energy = sum(at(phi, n) for n in range(len(pairs)))
-        force = [sum(at(slope, n) * vecs[n][c] for n in range(len(pairs))) for c in range(3)]
-        sums[i_key(i)].append((energy, force))
-        yield
-
-    sums = {}
-    keys = []
-
-    def i_key(i):
-        return [k for k, v in keys if v is i][0]
-
-    def run(items, offset):
-        gens = [work(i, p) for i, p in items]
-        for step in range(9 + offset * (len(gens) - 1)):
-            for g, gen in enumerate(gens):
-                if 0 <= step - offset * g < 9:
-                    next(gen)
-
-    def body(k, carry):
-        sums.clear()
-        keys.clear()
-        items = []
         for a in range(group):
             i = k * group + a
-            keys.append((a, i))
-            sums[a] = []
-            per = count // split
-            for h in range(split):
-                items.append((i, range(h * per, (h + 1) * per)))
-        run(items, offset)
-        for a, i in keys:
-            energy = sum(v[0] for v in sums[a])
-            energy_ref[pl.ds(i, 1), :] = 0.5 * energy
+            own = [pool_ref[c, pl.ds(i, 1), :] for c in range(3)]
+            for n in range(count):
+                idx = nb_ref[n, i]
+                vec = [pool_ref[c, pl.ds(idx, 1), :] + (bond_ref[c, n, i] - own[c]) for c in range(3)]
+                vecs.append(vec)
+                rows.append((vec[0] * vec[0] + vec[1] * vec[1] + vec[2] * vec[2]) * SCALE)
+        t = jnp.concatenate(rows, axis=1) - jnp.concatenate([muc_ref[...]] * (group * count), axis=1)
+        basis = jnp.exp2(-(t * t))
+        bt = basis * t
+        first = jnp.tanh(dot(w1a[...], jnp.concatenate([basis.astype(bf16), ones], axis=0)))
+        second = jnp.tanh(dot(w2a[...], jnp.concatenate([first.astype(bf16), ones], axis=0)))
+        slack = (1.0 - second * second).astype(bf16)
+        mixed = dot(w2o[...], jnp.concatenate([slack, second.astype(bf16)], axis=0))
+        phi = mixed[128:136]
+        back1 = (mixed[:128] * (1.0 - first * first)).astype(bf16)
+        slope = jnp.sum(dot(w1_ref[...], back1) * bt, axis=0, keepdims=True)
+        for a in range(group):
+            i = k * group + a
+            places = range(a * count, (a + 1) * count)
+            energy_ref[pl.ds(i, 1), :] = 0.5 * jnp.sum(sum(at(phi, n) for n in places), axis=0, keepdims=True)
             for c in range(3):
-                force_ref[c, pl.ds(i, 1), :] = sum(v[1][c] for v in sums[a]) * (-4.0 / (OMEGA * OMEGA * SCALE))
+                force_ref[c, pl.ds(i, 1), :] = sum(at(slope, n) * vecs[n][c] for n in places) * (-4.0 / (OMEGA * OMEGA * SCALE))
         return carry
 
     lax.fori_loop(0, atoms // group, body, 0)
 
 
-def pair_stage(pool, bond, nb, w1, b1, w2, b2, ow, group=2, split=1, offset=0):
+def pair_stage(pool, bond, nb, w1, b1, w2, b2, ow, group=2):
     atoms = bond.shape[1]
     samples = pool.shape[2]
     V = pl.BlockSpec(memory_space=pltpu.VMEM)
     S = pl.BlockSpec(memory_space=pltpu.SMEM)
     f32, bf16 = jnp.float32, jnp.bfloat16
     return pl.pallas_call(
-        functools.partial(pair_kernel, group, split, offset),
+        functools.partial(pair_kernel, group),
         out_shape=(jax.ShapeDtypeStruct((atoms, samples), f32), jax.ShapeDtypeStruct((3, atoms, samples), f32)),
         in_specs=[S, S, V, V, V, V, V, V],
         out_specs=(V, V),
-        scratch_shapes=[pltpu.VMEM((128, 128), f32)] * 2 + [pltpu.VMEM((128, 144), bf16)] * 2,
+        scratch_shapes=[pltpu.VMEM((128, 128), f32)] + [pltpu.VMEM((128, 144), bf16)] * 2 + [pltpu.VMEM((144, 256), bf16)],
         compiler_params=pltpu.CompilerParams(vmem_limit_bytes=16 * 2**20),
         name="pairs",
     )(nb.T, bond.transpose(0, 2, 1), pool, w1, b1, w2, b2, ow)

time: 65 us -> 61.5 us (0.946)
  Pallas kernels: 63.4 us -> 59.9 us
    pallas_call x1, Pallas kernels: 25.8 us -> 22.4 us  [pair_stage(): pl.pallas_call(functools.partial(pair_kernel, group), out_shape=(jax.Shap...]
where the time goes in v3:
time: 61.5 us; the launch traced here: 60.7 us
  Pallas kernels  59.9 us (97%)
  between operations  0.75 us (1%)
    pallas_call x1, Pallas kernels, displacement_pool(): pl.pallas_call(displacement_kernel, out_shape=jax.ShapeDtypeStruct((3, 17...  37.5 us
    pallas_call x1, Pallas kernels, pair_stage(): pl.pallas_call(functools.partial(pair_kernel, group), out_shape=(jax.Shap...  22.4 us

profile of v3, /device:TPU:0, one launch (start us, length us, event | category | flops | bytes accessed | tf_op | source)
XLA Modules:
  0.0 60.7 jit_solution(10487969551173863832)
XLA Ops:
  0.6 0.0 copy-start.6
  0.6 0.0 copy-start.5
  0.7 0.0 copy-start.1
  0.7 0.0 copy-start.4
  0.7 0.0 copy-start
  0.7 0.0 copy-start.3
  0.7 0.0 copy-start.2
  0.7 37.5 %displacements.1.pool_ref = f32[3,176,128]{2,1,0:T(8,128)S(1)} custom-call(s32[1,16]{1,0:T(1,128)} %sent_hbm.1, bf16[8,2,96,6144]{3,2,1,0:T(8,128)(2,1)} %bitcast.5, bf16[768,128]{1,0:T(8,128)(2,1)} %normals_ref.1), custom_call_target="tpu_custom_call" | custom-call | tf_op jit(solution)/shard_map/displacements/pallas_call | solution.py:229
  38.2 0.0 copy-done.6
  38.3 0.0 copy-done.5
  38.3 0.0 copy-done.1
  38.3 0.0 copy-done.4
  38.3 0.0 copy-done
  38.3 0.0 copy-done.3
  38.3 0.0 copy-done.2
  38.3 22.4 %pairs.1 = (f32[32,128]{1,0:T(8,128)}, f32[3,32,128]{2,1,0:T(8,128)}) custom-call(s32[12,32]{1,0:T(8,128)S(1)} %bitcast.4, f32[3,12,32]{2,1,0:T(8,128)S(1)} %bitcast.3, f32[3,176,128]{2,1,0:T(8,128)S(1)} %displacements.1.pool_ref, bf16[128,128]{1,0:T(8,128)(2,1)S(1)} %copy-done, f32[128]{0:T(128)S(1)} %copy-done.4, bf16[128,128]{1,0:T(8,128)(2,1)S(1)} %copy-done.1, ...), custom_call_target="tpu_custom_call" | custom-call | tf_op jit(solution)/shard_map/pairs/pallas_call | solution.py:325
Async XLA Ops:
  0.6 37.6 %copy-start.6 = (f32[128]{0:T(128)S(1)}, f32[128]{0:T(128)}, u32[]{:S(2)}) copy-start(f32[128]{0:T(128)} %ow_ref.1) | copy-start | bytes 1540
  0.6 37.6 %copy-start.5 = (f32[128]{0:T(128)S(1)}, f32[128]{0:T(128)}, u32[]{:S(2)}) copy-start(f32[128]{0:T(128)} %b2_ref.1) | copy-start | bytes 1540
  0.7 37.6 %copy-start.1 = (bf16[128,128]{1,0:T(8,128)(2,1)S(1)}, bf16[128,128]{1,0:T(8,128)(2,1)}, u32[]{:S(2)}) copy-start(bf16[128,128]{1,0:T(8,128)(2,1)} %w2_ref.1) | copy-start | bytes 98308
  0.7 37.6 %copy-start.4 = (f32[128]{0:T(128)S(1)}, f32[128]{0:T(128)}, u32[]{:S(2)}) copy-start(f32[128]{0:T(128)} %b1_ref.1) | copy-start | bytes 1540
  0.7 37.6 %copy-start = (bf16[128,128]{1,0:T(8,128)(2,1)S(1)}, bf16[128,128]{1,0:T(8,128)(2,1)}, u32[]{:S(2)}) copy-start(bf16[128,128]{1,0:T(8,128)(2,1)} %w1_ref.1) | copy-start | bytes 98308
  0.7 37.6 %copy-start.3 = (s32[32,12]{0,1:T(8,128)S(1)}, s32[32,12]{0,1:T(8,128)}, u32[]{:S(2)}) copy-start(s32[32,12]{0,1:T(8,128)} %param.13) | copy-start | bytes 4612
  0.7 37.6 %copy-start.2 = (f32[3,32,12]{1,2,0:T(8,128)S(1)}, f32[3,32,12]{1,2,0:T(8,128)}, u32[]{:S(2)}) copy-start(f32[3,32,12]{1,2,0:T(8,128)} %param.12) | copy-start | bytes 13828

commit v4 on v3

--- a/solution.py
+++ b/solution.py
@@ -25,7 +25,8 @@
     xp, xm, x2 = at_x(1), at_x(3), at_x(2)
     order = [p, xm, xp, other(p), x2, other(xm), other(xp), other(x2)]
     depth = normals_ref.shape[0]
-    half = depth // 2
+    third, sixth = depth // 3, depth // 6
+    pieces_at = ((0, third), (third, sixth), (third + sixth, sixth), (2 * third, third))
 
     own = pltpu.make_async_copy(normals_ref, nbuf.at[p], nsem)
     own.start()
@@ -54,7 +55,8 @@
     sends = []
 
     def part(place, h):
-        return nbuf.at[place, pl.ds(h * half, half)]
+        start, size = pieces_at[h]
+        return nbuf.at[place, pl.ds(start, size)]
 
     def push(place, h, device):
         n = len(sends)
@@ -67,62 +69,70 @@
 
     to_xp, to_xm, to_y = (xp, q), (xm, q), (other(p), q)
     own.wait()
-    push(p, 0, to_xp)
-    push(p, 1, to_xm)
-    push(p, 0, to_y)
-    push(p, 1, to_xp)
-    push(p, 0, to_xm)
-    push(p, 1, to_y)
-
-    def product(k, part):
-        weights = nbuf[order[k]]
-        out = jnp.dot(fbuf[k, part].reshape(768, depth), weights, preferred_element_type=jnp.float32).reshape(8, 96, 128)
-        acc[part] = out if k == 0 else acc[part] + out
-
-    def multiply(k):
+    for a, b, c in ((0, 3, 0), (1, 2, 3), (2, 1, 1), (3, 0, 2)):
+        push(p, a, to_xp)
+        push(p, b, to_xm)
+        push(p, c, to_y)
+
+    def product(cuts, part, first=False):
+        left = jnp.concatenate([fbuf[k, part, :, :, start:start + size].reshape(768, size) for k, start, size in cuts], axis=1)
+        right = jnp.concatenate([nbuf[order[k], start:start + size] for k, start, size in cuts], axis=0)
+        out = jnp.dot(left, right, preferred_element_type=jnp.float32).reshape(8, 96, 128)
+        acc[part] = out if first else acc[part] + out
+
+    def multiply(cuts, first=False):
+        def half_rows(part, carry):
+            product(cuts, part, first)
+            return carry
+
+        lax.fori_loop(0, 2, half_rows, 0)
+
+    def chunk(k):
         for copy in loads[k]:
             copy.wait()
-
-        def half_rows(part, carry):
-            product(k, part)
-            return carry
-
-        lax.fori_loop(0, 2, half_rows, 0)
-
-    multiply(0)
-    arrive(xm, 0)
-    push(xm, 0, to_xp)
-    arrive(xp, 1)
-    push(xp, 1, to_xm)
+        multiply([(k, 0, depth)], k == 0)
+
+    def last(start):
+        return [(k, start, third) for k in (5, 6, 7)]
+
+    chunk(0)
     for h in (0, 1):
+        arrive(xm, h)
+        push(xm, h, to_xp)
+        arrive(xp, 3 - h)
+        push(xp, 3 - h, to_xm)
+    for h in (0, 3, 1, 2):
         arrive(other(p), h)
         push(other(p), h, to_xp)
         push(other(p), h, to_xm)
-    arrive(xm, 1)
-    multiply(1)
-    arrive(xp, 0)
-    multiply(2)
+    for h in (2, 3):
+        arrive(xm, h)
+        arrive(xp, 3 - h)
     pl.semaphore_wait(y_ready, 3)
     for device in z_ring:
         pl.semaphore_signal(z_ready, inc=1, device_id=device, device_id_type=MESH)
-    arrive(x2, 0)
-    push(x2, 0, to_y)
-    arrive(x2, 1)
-    push(x2, 1, to_y)
-    multiply(3)
-    multiply(4)
+    chunk(1)
+    for h in (0, 3):
+        arrive(x2, h)
+        push(x2, h, to_y)
+    chunk(2)
+    for h in (1, 2):
+        arrive(x2, h)
+        push(x2, h, to_y)
+    chunk(3)
+    chunk(4)
     pl.semaphore_wait(z_ready, 3)
     pl.semaphore_signal(core_ready, inc=1, device_id=partner, device_id_type=MESH)
-    for h in (0, 1):
-        arrive(other(xm), h)
-    multiply(5)
-    for h in (0, 1):
-        arrive(other(xp), h)
-    multiply(6)
-    for h in (0, 1):
-        arrive(other(x2), h)
-    for copy in loads[7]:
-        copy.wait()
+    for k in (5, 6, 7):
+        for copy in loads[k]:
+            copy.wait()
+    for h, start in ((0, 0), (3, 2 * third)):
+        for place in (other(xm), other(xp), other(x2)):
+            arrive(place, h)
+        multiply(last(start))
+    for h in (1, 2):
+        for place in (other(xm), other(xp), other(x2)):
+            arrive(place, h)
     group = q // 2
 
     def ahead(step):
@@ -133,7 +143,7 @@
     def swap(m):
         return remote(acc.at[0, m], pbuf.at[m], psend.at[m], precv.at[m], partner)
 
-    product(7, 0)
+    product(last(third), 0)
 
     def swap_out(step, carry):
         swap(ahead(step)).start()
@@ -141,7 +151,7 @@
 
     lax.fori_loop(0, 7, swap_out, 0)
     swap(group).start()
-    product(7, 1)
+    product(last(third), 1)
     pl.semaphore_wait(core_ready, 1)
 
     def spread(step, carry):
@@ -189,15 +199,12 @@
         for h in range(16):
             hsend[c, pl.ds(h, 1)] = disp[pl.ds(c * 32 + sent_ref[0, h], 1), :]
     halos = []
-    for u in (-1, 0, 1):
-        for v in (-1, 0, 1):
-            slot = (u + 1) * 3 + v + 1
-            if u == 0 and v == 0:
-                pool[:, 32 + 16 * slot:48 + 16 * slot] = hsend[...]
-                continue
-            device = (lax.rem(p - u + 8, 8), lax.rem(q - v + 16, 16))
-            halos.append(remote(hsend, pool.at[:, pl.ds(32 + 16 * slot, 16)], hsends.at[slot], hrecv.at[slot], device))
-            halos[-1].start()
+    pool[:, 32 + 64:48 + 64] = hsend[...]
+    for u, v in ((-1, -1), (1, 1), (-1, 1), (1, -1), (-1, 0), (1, 0), (0, -1), (0, 1)):
+        slot = (u + 1) * 3 + v + 1
+        device = (lax.rem(p - u + 8, 8), lax.rem(q - v + 16, 16))
+        halos.append(remote(hsend, pool.at[:, pl.ds(32 + 16 * slot, 16)], hsends.at[slot], hrecv.at[slot], device))
+        halos[-1].start()
     for copy in halos:
         copy.wait_recv()
     pool_ref[...] = pool[...]
@@ -236,7 +243,7 @@
             pltpu.VMEM((2, 8, 96, samples), f32), pltpu.VMEM((8, 96, samples), f32),
             pltpu.VMEM((8, 6, 16, samples), f32), pltpu.VMEM((8, 6, 16, samples), f32),
             pltpu.VMEM((96, samples), f32), pltpu.VMEM((3, 16, samples), f32), pltpu.VMEM((3, 176, samples), f32),
-            dma((8, 2)), dma, dma((14,)), dma((8, 2)), dma((8,)), dma((8,)), dma((8,)), dma((8,)), dma((6,)), dma((6,)), dma((9,)), dma((9,)),
+            dma((8, 2)), dma, dma((28,)), dma((8, 4)), dma((8,)), dma((8,)), dma((8,)), dma((8,)), dma((6,)), dma((6,)), dma((9,)), dma((9,)),
             regular, regular, regular, pltpu.SMEM((1, 16), jnp.int32), dma,
         ],
         compiler_params=pltpu.CompilerParams(collective_id=0, has_side_effects=True, vmem_limit_bytes=48 * 2**20),
@@ -264,8 +271,8 @@
     return jnp.concatenate([weights_t, extra.astype(jnp.bfloat16)], axis=1)[:, :144]
 
 
-def pair_kernel(group, nb_ref, bond_ref, pool_ref, w1_ref, b1_ref, w2_ref, b2_ref, ow_ref,
-                energy_ref, force_ref, muc_ref, w1a, w2a, w2o):
+def pair_kernel(pairs, nb_ref, bond_ref, pool_ref, w1_ref, b1_ref, w2_ref, b2_ref, ow_ref,
+                energy_ref, force_ref, ow_s, muc_ref, w1a, w2a, vec_s, sq_s, phi_s):
     atoms = energy_ref.shape[0]
     count = nb_ref.shape[0]
     bf16, f32 = jnp.bfloat16, jnp.float32
@@ -273,61 +280,71 @@
     muc_ref[...] = lax.broadcasted_iota(jnp.int32, (128, 128), 0).astype(f32) * (MU * SCALE)
     w1a[...] = beside(w1_ref[...].T, spread(b1_ref).T)
     w2a[...] = beside(w2_ref[...].T, spread(b2_ref).T)
-    scaled = (w2_ref[...].astype(f32) * spread(ow_ref)).astype(bf16)
-    line = lax.broadcasted_iota(jnp.int32, (16, 128), 0)
-    high, middle, low = [v.astype(f32)[:16] for v in pieces(spread(ow_ref))]
-    read = jnp.where(line == 0, high, jnp.where(line == 1, middle, jnp.where(line == 2, low, 0.0))).astype(bf16)
-    w2o[...] = jnp.concatenate([
-        jnp.concatenate([scaled, jnp.zeros((128, 128), bf16)], axis=1),
-        jnp.concatenate([jnp.zeros((16, 128), bf16), read], axis=1)], axis=0)
+    ow_s[...] = spread(ow_ref).T
     dot = functools.partial(jnp.dot, preferred_element_type=f32)
-    wide = group * count * 128
-    ones = jnp.where(lax.broadcasted_iota(jnp.int32, (16, wide), 0) < 3, 1.0, 0.0).astype(bf16)
     at = lambda v, n: v[:, n * 128:(n + 1) * 128]
 
+    def gather(n, carry):
+        base = pl.multiple_of(n * atoms, atoms)
+        for i in range(atoms):
+            idx = nb_ref[n, i]
+            for c in range(3):
+                vec_s[c, pl.ds(base + i, 1), :] = pool_ref[c, pl.ds(idx, 1), :] + bond_ref[c, n, i]
+        square = jnp.zeros((atoms, 128), f32)
+        for c in range(3):
+            vec = vec_s[c, pl.ds(base, atoms), :] - pool_ref[c, 0:atoms, :]
+            vec_s[c, pl.ds(base, atoms), :] = vec
+            square = square + vec * vec
+        sq_s[pl.ds(base, atoms), :] = square * SCALE
+        return carry
+
+    lax.fori_loop(0, count, gather, 0)
+    ones = jnp.where(lax.broadcasted_iota(jnp.int32, (16, pairs * 128), 0) < 3, 1.0, 0.0).astype(bf16)
+
     def body(k, carry):
-        rows, vecs = [], []
-        for a in range(group):
-            i = k * group + a
-            own = [pool_ref[c, pl.ds(i, 1), :] for c in range(3)]
-            for n in range(count):
-                idx = nb_ref[n, i]
-                vec = [pool_ref[c, pl.ds(idx, 1), :] + (bond_ref[c, n, i] - own[c]) for c in range(3)]
-                vecs.append(vec)
-                rows.append((vec[0] * vec[0] + vec[1] * vec[1] + vec[2] * vec[2]) * SCALE)
-        t = jnp.concatenate(rows, axis=1) - jnp.concatenate([muc_ref[...]] * (group * count), axis=1)
+        base = pl.multiple_of(k * pairs, pairs)
+        sq = jnp.concatenate([sq_s[pl.ds(base + n, 1), :] for n in range(pairs)], axis=1)
+        t = sq - jnp.concatenate([muc_ref[...]] * pairs, axis=1)
+        ow = jnp.concatenate([ow_s[...]] * (pairs), axis=1)
         basis = jnp.exp2(-(t * t))
         bt = basis * t
         first = jnp.tanh(dot(w1a[...], jnp.concatenate([basis.astype(bf16), ones], axis=0)))
         second = jnp.tanh(dot(w2a[...], jnp.concatenate([first.astype(bf16), ones], axis=0)))
-        slack = (1.0 - second * second).astype(bf16)
-        mixed = dot(w2o[...], jnp.concatenate([slack, second.astype(bf16)], axis=0))
-        phi = mixed[128:136]
-        back1 = (mixed[:128] * (1.0 - first * first)).astype(bf16)
+        so = second * ow
+        slack = (ow - second * so).astype(bf16)
+        phi = jnp.sum(so, axis=0, keepdims=True)
+        back1 = (dot(w2_ref[...], slack) * (1.0 - first * first)).astype(bf16)
         slope = jnp.sum(dot(w1_ref[...], back1) * bt, axis=0, keepdims=True)
-        for a in range(group):
-            i = k * group + a
-            places = range(a * count, (a + 1) * count)
-            energy_ref[pl.ds(i, 1), :] = 0.5 * jnp.sum(sum(at(phi, n) for n in places), axis=0, keepdims=True)
-            for c in range(3):
-                force_ref[c, pl.ds(i, 1), :] = sum(at(slope, n) * vecs[n][c] for n in places) * (-4.0 / (OMEGA * OMEGA * SCALE))
-        return carry
-
-    lax.fori_loop(0, atoms // group, body, 0)
-
-
-def pair_stage(pool, bond, nb, w1, b1, w2, b2, ow, group=2):
+        for n in range(pairs):
+            phi_s[pl.ds(base + n, 1), :] = at(phi, n)
+            sq_s[pl.ds(base + n, 1), :] = at(slope, n)
+        return carry
+
+    lax.fori_loop(0, count * atoms // pairs, body, 0)
+    energy = jnp.zeros((atoms, 128), f32)
+    force = [jnp.zeros((atoms, 128), f32) for _ in range(3)]
+    for n in range(count):
+        rows = pl.ds(n * atoms, atoms)
+        energy = energy + phi_s[rows, :]
+        for c in range(3):
+            force[c] = force[c] + sq_s[rows, :] * vec_s[c, rows, :]
+    energy_ref[...] = 0.5 * energy
+    for c in range(3):
+        force_ref[c] = force[c] * (-4.0 / (OMEGA * OMEGA * SCALE))
+
+
+def pair_stage(pool, bond, nb, w1, b1, w2, b2, ow, pairs=24):
     atoms = bond.shape[1]
     samples = pool.shape[2]
     V = pl.BlockSpec(memory_space=pltpu.VMEM)
     S = pl.BlockSpec(memory_space=pltpu.SMEM)
     f32, bf16 = jnp.float32, jnp.bfloat16
     return pl.pallas_call(
-        functools.partial(pair_kernel, group),
+        functools.partial(pair_kernel, pairs),
         out_shape=(jax.ShapeDtypeStruct((atoms, samples), f32), jax.ShapeDtypeStruct((3, atoms, samples), f32)),
         in_specs=[S, S, V, V, V, V, V, V],
         out_specs=(V, V),
-        scratch_shapes=[pltpu.VMEM((128, 128), f32)] + [pltpu.VMEM((128, 144), bf16)] * 2 + [pltpu.VMEM((144, 256), bf16)],
+        scratch_shapes=[pltpu.VMEM((128, 128), f32)] * 2 + [pltpu.VMEM((128, 144), bf16)] * 2 + [pltpu.VMEM((3, 384, samples), f32), pltpu.VMEM((384, samples), f32), pltpu.VMEM((384, samples), f32)],
         compiler_params=pltpu.CompilerParams(vmem_limit_bytes=16 * 2**20),
         name="pairs",
     )(nb.T, bond.transpose(0, 2, 1), pool, w1, b1, w2, b2, ow)

time: 61.5 us -> 64.1 us (1.042)
  Pallas kernels: 59.9 us -> 62.8 us
    pallas_call x1, Pallas kernels: 22.4 us -> 25.3 us  [pair_stage(): pl.pallas_call(functools.partial(pair_kernel, pairs), out_shape=(jax.Shap...]
where the time goes in v4:
time: 64.1 us; the launch traced here: 63.6 us
  Pallas kernels  62.8 us (98%)
  between operations  0.75 us (1%)
    pallas_call x1, Pallas kernels, displacement_pool(): pl.pallas_call(displacement_kernel, out_shape=jax.ShapeDtypeStruct((3, 17...  37.5 us
    pallas_call x1, Pallas kernels, pair_stage(): pl.pallas_call(functools.partial(pair_kernel, pairs), out_shape=(jax.Shap...  25.3 us

profile of v4, /device:TPU:0, one launch (start us, length us, event | category | flops | bytes accessed | tf_op | source)
XLA Modules:
  0.0 63.6 jit_solution(4422363232614065856)
XLA Ops:
  0.6 0.0 copy-start.6
  0.6 0.0 copy-start.5
  0.7 0.0 copy-start.1
  0.7 0.0 copy-start.4
  0.7 0.0 copy-start
  0.7 0.0 copy-start.3
  0.7 0.0 copy-start.2
  0.7 37.5 %displacements.1.pool_ref = f32[3,176,128]{2,1,0:T(8,128)S(1)} custom-call(s32[1,16]{1,0:T(1,128)} %sent_hbm.1, bf16[8,2,96,6144]{3,2,1,0:T(8,128)(2,1)} %bitcast.5, bf16[768,128]{1,0:T(8,128)(2,1)} %normals_ref.1), custom_call_target="tpu_custom_call" | custom-call | tf_op jit(solution)/shard_map/displacements/pallas_call | solution.py:236
  38.2 0.0 copy-done.6
  38.2 0.0 copy-done.5
  38.2 0.0 copy-done.1
  38.2 0.0 copy-done.4
  38.3 0.0 copy-done
  38.3 0.0 copy-done.3
  38.3 0.0 copy-done.2
  38.3 25.3 %pairs.1 = (f32[32,128]{1,0:T(8,128)}, f32[3,32,128]{2,1,0:T(8,128)}) custom-call(s32[12,32]{1,0:T(8,128)S(1)} %bitcast.4, f32[3,12,32]{2,1,0:T(8,128)S(1)} %bitcast.3, f32[3,176,128]{2,1,0:T(8,128)S(1)} %displacements.1.pool_ref, bf16[128,128]{1,0:T(8,128)(2,1)S(1)} %copy-done, f32[128]{0:T(128)S(1)} %copy-done.4, bf16[128,128]{1,0:T(8,128)(2,1)S(1)} %copy-done.1, ...), custom_call_target="tpu_custom_call" | custom-call | tf_op jit(solution)/shard_map/pairs/pallas_call | solution.py:342
Async XLA Ops:
  0.6 37.6 %copy-start.6 = (f32[128]{0:T(128)S(1)}, f32[128]{0:T(128)}, u32[]{:S(2)}) copy-start(f32[128]{0:T(128)} %ow_ref.1) | copy-start | bytes 1540
  0.6 37.6 %copy-start.5 = (f32[128]{0:T(128)S(1)}, f32[128]{0:T(128)}, u32[]{:S(2)}) copy-start(f32[128]{0:T(128)} %b2_ref.1) | copy-start | bytes 1540
  0.7 37.6 %copy-start.1 = (bf16[128,128]{1,0:T(8,128)(2,1)S(1)}, bf16[128,128]{1,0:T(8,128)(2,1)}, u32[]{:S(2)}) copy-start(bf16[128,128]{1,0:T(8,128)(2,1)} %w2_ref.1) | copy-start | bytes 98308
  0.7 37.6 %copy-start.4 = (f32[128]{0:T(128)S(1)}, f32[128]{0:T(128)}, u32[]{:S(2)}) copy-start(f32[128]{0:T(128)} %b1_ref.1) | copy-start | bytes 1540
  0.7 37.6 %copy-start = (bf16[128,128]{1,0:T(8,128)(2,1)S(1)}, bf16[128,128]{1,0:T(8,128)(2,1)}, u32[]{:S(2)}) copy-start(bf16[128,128]{1,0:T(8,128)(2,1)} %w1_ref.1) | copy-start | bytes 98308
  0.7 37.6 %copy-start.3 = (s32[32,12]{0,1:T(8,128)S(1)}, s32[32,12]{0,1:T(8,128)}, u32[]{:S(2)}) copy-start(s32[32,12]{0,1:T(8,128)} %param.13) | copy-start | bytes 4612
  0.7 37.6 %copy-start.2 = (f32[3,32,12]{1,2,0:T(8,128)S(1)}, f32[3,32,12]{1,2,0:T(8,128)}, u32[]{:S(2)}) copy-start(f32[3,32,12]{1,2,0:T(8,128)} %param.12) | copy-start | bytes 13828

commit v5 on v4

--- a/solution.py
+++ b/solution.py
@@ -284,21 +284,20 @@
     dot = functools.partial(jnp.dot, preferred_element_type=f32)
     at = lambda v, n: v[:, n * 128:(n + 1) * 128]
 
-    def gather(n, carry):
-        base = pl.multiple_of(n * atoms, atoms)
+    bonds = [bond_ref[c].T for c in range(3)]
+    for n in range(count):
+        base = n * atoms
         for i in range(atoms):
             idx = nb_ref[n, i]
             for c in range(3):
-                vec_s[c, pl.ds(base + i, 1), :] = pool_ref[c, pl.ds(idx, 1), :] + bond_ref[c, n, i]
+                vec_s[c, base + i:base + i + 1, :] = pool_ref[c, pl.ds(idx, 1), :]
         square = jnp.zeros((atoms, 128), f32)
         for c in range(3):
-            vec = vec_s[c, pl.ds(base, atoms), :] - pool_ref[c, 0:atoms, :]
-            vec_s[c, pl.ds(base, atoms), :] = vec
+            vec = bonds[c][:, n:n + 1] + vec_s[c, base:base + atoms, :] - pool_ref[c, 0:atoms, :]
+            vec_s[c, base:base + atoms, :] = vec
             square = square + vec * vec
-        sq_s[pl.ds(base, atoms), :] = square * SCALE
-        return carry
-
-    lax.fori_loop(0, count, gather, 0)
+        sq_s[base:base + atoms, :] = square * SCALE
+
     ones = jnp.where(lax.broadcasted_iota(jnp.int32, (16, pairs * 128), 0) < 3, 1.0, 0.0).astype(bf16)
 
     def body(k, carry):
@@ -342,7 +341,7 @@
     return pl.pallas_call(
         functools.partial(pair_kernel, pairs),
         out_shape=(jax.ShapeDtypeStruct((atoms, samples), f32), jax.ShapeDtypeStruct((3, atoms, samples), f32)),
-        in_specs=[S, S, V, V, V, V, V, V],
+        in_specs=[S, V, V, V, V, V, V, V],
         out_specs=(V, V),
         scratch_shapes=[pltpu.VMEM((128, 128), f32)] * 2 + [pltpu.VMEM((128, 144), bf16)] * 2 + [pltpu.VMEM((3, 384, samples), f32), pltpu.VMEM((384, samples), f32), pltpu.VMEM((384, samples), f32)],
         compiler_params=pltpu.CompilerParams(vmem_limit_bytes=16 * 2**20),

time: 64.1 us -> 63.1 us (0.984)
  Pallas kernels: 62.8 us -> 61.9 us
    pallas_call x1, Pallas kernels: 25.3 us -> 24.4 us  [pair_stage(): pl.pallas_call(functools.partial(pair_kernel, pairs), out_shape=(jax.Shap...]
where the time goes in v5:
time: 63.1 us; the launch traced here: 62.7 us
  Pallas kernels  61.9 us (98%)
  between operations  0.75 us (1%)
    pallas_call x1, Pallas kernels, displacement_pool(): pl.pallas_call(displacement_kernel, out_shape=jax.ShapeDtypeStruct((3, 17...  37.5 us
    pallas_call x1, Pallas kernels, pair_stage(): pl.pallas_call(functools.partial(pair_kernel, pairs), out_shape=(jax.Shap...  24.4 us

profile of v5, /device:TPU:0, one launch (start us, length us, event | category | flops | bytes accessed | tf_op | source)
XLA Modules:
  0.0 62.7 jit_solution(342669851551870922)
XLA Ops:
  0.6 0.0 copy-start.6
  0.6 0.0 copy-start.5
  0.7 0.0 copy-start.1
  0.7 0.0 copy-start.4
  0.7 0.0 copy-start
  0.7 0.0 copy-start.3
  0.7 0.0 copy-start.2
  0.7 37.5 %displacements.1.pool_ref = f32[3,176,128]{2,1,0:T(8,128)S(1)} custom-call(s32[1,16]{1,0:T(1,128)} %sent_hbm.1, bf16[8,2,96,6144]{3,2,1,0:T(8,128)(2,1)} %bitcast.5, bf16[768,128]{1,0:T(8,128)(2,1)} %normals_ref.1), custom_call_target="tpu_custom_call" | custom-call | tf_op jit(solution)/shard_map/displacements/pallas_call | solution.py:236
  38.2 0.0 copy-done.6
  38.2 0.0 copy-done.5
  38.2 0.0 copy-done.1
  38.2 0.0 copy-done.4
  38.3 0.0 copy-done
  38.3 0.0 copy-done.3
  38.3 0.0 copy-done.2
  38.3 24.4 %pairs.1 = (f32[32,128]{1,0:T(8,128)}, f32[3,32,128]{2,1,0:T(8,128)}) custom-call(s32[12,32]{1,0:T(8,128)S(1)} %bitcast.4, f32[3,12,32]{2,1,0:T(8,128)S(1)} %bitcast.3, f32[3,176,128]{2,1,0:T(8,128)S(1)} %displacements.1.pool_ref, bf16[128,128]{1,0:T(8,128)(2,1)S(1)} %copy-done, f32[128]{0:T(128)S(1)} %copy-done.4, bf16[128,128]{1,0:T(8,128)(2,1)S(1)} %copy-done.1, ...), custom_call_target="tpu_custom_call" | custom-call | tf_op jit(solution)/shard_map/pairs/pallas_call | solution.py:341
Async XLA Ops:
  0.6 37.6 %copy-start.6 = (f32[128]{0:T(128)S(1)}, f32[128]{0:T(128)}, u32[]{:S(2)}) copy-start(f32[128]{0:T(128)} %ow_ref.1) | copy-start | bytes 1540
  0.6 37.6 %copy-start.5 = (f32[128]{0:T(128)S(1)}, f32[128]{0:T(128)}, u32[]{:S(2)}) copy-start(f32[128]{0:T(128)} %b2_ref.1) | copy-start | bytes 1540
  0.7 37.6 %copy-start.1 = (bf16[128,128]{1,0:T(8,128)(2,1)S(1)}, bf16[128,128]{1,0:T(8,128)(2,1)}, u32[]{:S(2)}) copy-start(bf16[128,128]{1,0:T(8,128)(2,1)} %w2_ref.1) | copy-start | bytes 98308
  0.7 37.6 %copy-start.4 = (f32[128]{0:T(128)S(1)}, f32[128]{0:T(128)}, u32[]{:S(2)}) copy-start(f32[128]{0:T(128)} %b1_ref.1) | copy-start | bytes 1540
  0.7 37.6 %copy-start = (bf16[128,128]{1,0:T(8,128)(2,1)S(1)}, bf16[128,128]{1,0:T(8,128)(2,1)}, u32[]{:S(2)}) copy-start(bf16[128,128]{1,0:T(8,128)(2,1)} %w1_ref.1) | copy-start | bytes 98308
  0.7 37.6 %copy-start.3 = (s32[32,12]{0,1:T(8,128)S(1)}, s32[32,12]{0,1:T(8,128)}, u32[]{:S(2)}) copy-start(s32[32,12]{0,1:T(8,128)} %param.13) | copy-start | bytes 4612
  0.7 37.6 %copy-start.2 = (f32[3,32,12]{1,2,0:T(8,128)S(1)}, f32[3,32,12]{1,2,0:T(8,128)}, u32[]{:S(2)}) copy-start(f32[3,32,12]{1,2,0:T(8,128)} %param.12) | copy-start | bytes 13828
